TPU v7x, 32 devices: a whole 2x2x4 slice. The times are simulated.
32 devices in a mesh: dp: 8 (over z, y), head: 4 (over x, core).
Axes of the slice: x: 2, y: 2, z: 4, core: 2. Of those that a mesh axis runs over, the one named last changes fastest.
Arguments:
- tokens: bfloat16 [2, 32, 512, 768], P(None, ('dp', 'head')), may hold values from -6 to 6
- lengths: int32 [2, 32], P(None, 'dp'), may hold values from 1 to 512, as said below
- cotangent: bfloat16 [2, 32, 512, 768], P(None, ('dp', 'head')), may hold values from -12 to 12
- qkv_weight: bfloat16 [768, 2304], P('dp', 'head'), may hold values from -0.3125 to 0.3125
- qv_shift: bfloat16 [12, 128], P('head', 'dp'), may hold values from -3 to 3
- proj_weight: bfloat16 [768, 768], P(('dp', 'head')), may hold values from -0.875 to 0.875
- proj_shift: bfloat16 [768], P(('dp', 'head')), may hold values from -3 to 3
- first_gain: bfloat16 [768], P(('dp', 'head')), may hold values from 0.5 to 1.5
- first_shift: bfloat16 [768], P(('dp', 'head')), may hold values from -1.75 to 1.75
- inner_weight: bfloat16 [768, 3072], P(('dp', 'head')), may hold values from -0.21875 to 0.21875
- inner_shift: bfloat16 [3072], P(('dp', 'head')), may hold values from -3 to 3
- outer_weight: bfloat16 [3072, 768], P(('dp', 'head')), may hold values from -0.21875 to 0.21875
- outer_shift: bfloat16 [768], P(('dp', 'head')), may hold values from -3 to 3
- second_gain: bfloat16 [768], P(('dp', 'head')), may hold values from 0.5 to 1.5
- second_shift: bfloat16 [768], P(('dp', 'head')), may hold values from -1.75 to 1.75
Outputs:
- layer_output: bfloat16 [2, 32, 512, 768], P(None, ('dp', 'head'))
- tokens_gradient: bfloat16 [2, 32, 512, 768], P(None, ('dp', 'head'))
- qkv_gradient: float32 [768, 2304], P('dp', 'head')
- qvshift_gradient: float32 [12, 128], P('head', 'dp')
- proj_gradient: float32 [768, 768], P(('dp', 'head'))
- projshift_gradient: float32 [768], P(('dp', 'head'))
- firstgain_gradient: float32 [768], P(('dp', 'head'))
- firstshift_gradient: float32 [768], P(('dp', 'head'))
- inner_gradient: float32 [768, 3072], P(('dp', 'head'))
- innershift_gradient: float32 [3072], P(('dp', 'head'))
- outer_gradient: float32 [3072, 768], P(('dp', 'head'))
- outershift_gradient: float32 [768], P(('dp', 'head'))
- secondgain_gradient: float32 [768], P(('dp', 'head'))
- secondshift_gradient: float32 [768], P(('dp', 'head'))
Inputs may be any that keep to these rules, and one draw needn't show every extreme that they name: lengths[m, s] is the number of live slots at the start of row s of micro-batch m; the other slots are padding. Lengths are mixed: some row has all 512 slots live, others about a third of them.
All inputs are finite; a program needn't handle non-finite values.
Results may differ from a plain program's by a relative error of at most 0.018.
Values may be sent and summed in bfloat16 or wider, within the bound.
No kernel may reach another device: no remote copies, remote signals or barrier semaphores. Data moves between devices by JAX's collectives and lax.ppermute only.
A program may use at most 192 MiB of HBM per device.

v0:
```python
import jax
import jax.numpy as jnp
from jax import lax
from jax.sharding import PartitionSpec as P

DH = 64
SLOTS = 512


EPSILON = 1e-12


def cut_along(value, dim, count):
    before, after = (value.shape[:dim], value.shape[dim + 1 :])
    return jnp.moveaxis(value.reshape(*before, count, -1, *after), dim, 0)


def sum_at_owner(value, axis, dim):
    count = lax.axis_size(axis)
    blocks = lax.all_to_all(cut_along(value, dim, count), axis, 0, 0, tiled=True)
    return jnp.sum(blocks.astype(jnp.float32), axis=0)


def layer_norm(hidden, scale_gain, offset):
    center = hidden - jnp.mean(hidden, axis=-1, keepdims=True)
    spread = jnp.mean(center * center, axis=-1, keepdims=True)
    return center * lax.rsqrt(spread + EPSILON) * scale_gain + offset


def gelu_exact(values):
    return jax.nn.gelu(values, approximate=False)


def attention_scores(queries, keyset, live_keys):
    scores = jnp.einsum(
        "sqhd,skhd->shqk", queries, keyset, preferred_element_type=jnp.float32
    ) * DH ** (-0.5)
    return jnp.where(live_keys[:, None, None, :], scores, -1e30)


def spread_grads(attn_terms, token_terms):
    attn_part = (
        sum_at_owner(attn_terms[0].astype(jnp.bfloat16), "dp", 0),
        sum_at_owner(attn_terms[1].astype(jnp.bfloat16), "dp", 1),
    )
    token_part = (
        lax.psum_scatter(token_terms[0], ("dp", "head"), scatter_dimension=0, tiled=True),
        lax.psum_scatter(token_terms[1], ("dp", "head"), scatter_dimension=0, tiled=True),
        lax.psum_scatter(token_terms[2], ("dp", "head"), scatter_dimension=0, tiled=True),
        lax.psum_scatter(token_terms[3], ("dp", "head"), scatter_dimension=0, tiled=True),
        lax.psum_scatter(token_terms[4], ("dp", "head"), scatter_dimension=0, tiled=True),
        lax.psum_scatter(token_terms[5], ("dp", "head"), scatter_dimension=0, tiled=True),
        lax.psum_scatter(token_terms[6], ("dp", "head"), scatter_dimension=0, tiled=True),
        lax.psum_scatter(token_terms[7], ("dp", "head"), scatter_dimension=0, tiled=True),
        lax.psum_scatter(token_terms[8], ("dp", "head"), scatter_dimension=0, tiled=True),
        lax.psum_scatter(token_terms[9], ("dp", "head"), scatter_dimension=0, tiled=True),
    )
    return (attn_part, token_part)


def add_terms(total, terms):
    if total is None:
        return terms
    return jax.tree.map(jnp.add, total, terms)


def on_device(
    tokens,
    lengths,
    cotangent,
    qkv_weight,
    qv_shift,
    proj_weight,
    proj_shift,
    first_gain,
    first_shift,
    inner_weight,
    inner_shift,
    outer_weight,
    outer_shift,
    second_gain,
    second_shift,
):
    micro_count, local_seq, slot_count, feature_count = tokens.shape
    local_heads = qv_shift.shape[0]
    position = lax.axis_index("head")
    full_seq = local_seq * lax.axis_size("head")
    slot_ids = jnp.arange(SLOTS, dtype=jnp.int32)
    row_count = local_seq * slot_count
    outputs = []
    input_grads = []
    attn_total = None
    token_total = None
    for micro_index in range(micro_count):
        local_qkv, local_shift = (
            lax.all_gather(qkv_weight, "dp", axis=0, tiled=True),
            lax.all_gather(qv_shift, "dp", axis=1, tiled=True),
        )
        (
            full_proj,
            full_proj_shift,
            gain_one,
            shift_one,
            full_inner,
            full_inner_shift,
            full_outer,
            full_outer_shift,
            gain_two,
            shift_two,
        ) = (
            lax.all_gather(proj_weight, ("dp", "head"), axis=0, tiled=True),
            lax.all_gather(proj_shift, ("dp", "head"), axis=0, tiled=True),
            lax.all_gather(first_gain, ("dp", "head"), axis=0, tiled=True),
            lax.all_gather(first_shift, ("dp", "head"), axis=0, tiled=True),
            lax.all_gather(inner_weight, ("dp", "head"), axis=0, tiled=True),
            lax.all_gather(inner_shift, ("dp", "head"), axis=0, tiled=True),
            lax.all_gather(outer_weight, ("dp", "head"), axis=0, tiled=True),
            lax.all_gather(outer_shift, ("dp", "head"), axis=0, tiled=True),
            lax.all_gather(second_gain, ("dp", "head"), axis=0, tiled=True),
            lax.all_gather(second_shift, ("dp", "head"), axis=0, tiled=True),
        )
        tokens_here = tokens[micro_index]
        gathered = lax.all_gather(tokens_here, "head", axis=0, tiled=True)
        length_here = lengths[micro_index]
        live_keys = slot_ids[None, :] < length_here[:, None]
        token_rows = gathered.reshape(full_seq * SLOTS, feature_count)
        packed = jnp.dot(token_rows, local_qkv, preferred_element_type=jnp.float32)
        packed = packed.reshape(full_seq, SLOTS, local_heads, 3, DH)
        shift_wide = local_shift.astype(jnp.float32)
        queries = (packed[:, :, :, 0, :] + shift_wide[:, :DH]).astype(jnp.bfloat16)
        keyset = packed[:, :, :, 1, :].astype(jnp.bfloat16)
        values = (packed[:, :, :, 2, :] + shift_wide[:, DH:]).astype(jnp.bfloat16)
        scores = attention_scores(queries, keyset, live_keys)
        highest = jnp.max(scores, axis=-1, keepdims=True)
        log_total = highest + jnp.log(jnp.sum(jnp.exp(scores - highest), axis=-1, keepdims=True))
        soft_low = jnp.exp(scores - log_total).astype(jnp.bfloat16)
        context = jnp.einsum(
            "shqk,skhd->sqhd", soft_low, values, preferred_element_type=jnp.float32
        )
        context = context.astype(jnp.bfloat16).reshape(full_seq, SLOTS, local_heads * DH)
        context_tok = lax.all_to_all(context, "head", split_axis=0, concat_axis=2, tiled=True)
        residual = tokens_here.reshape(row_count, feature_count).astype(jnp.float32)
        context_rows = context_tok.reshape(row_count, feature_count)
        attended = jnp.dot(
            context_rows, full_proj, preferred_element_type=jnp.float32
        ) + full_proj_shift.astype(jnp.float32)
        normed, first_pull = jax.vjp(
            layer_norm,
            residual + attended,
            gain_one.astype(jnp.float32),
            shift_one.astype(jnp.float32),
        )
        normed_low = normed.astype(jnp.bfloat16)
        inner_pre = jnp.dot(
            normed_low, full_inner, preferred_element_type=jnp.float32
        ) + full_inner_shift.astype(jnp.float32)
        active, gelu_pull = jax.vjp(gelu_exact, inner_pre)
        active_low = active.astype(jnp.bfloat16)
        outer_pre = jnp.dot(
            active_low, full_outer, preferred_element_type=jnp.float32
        ) + full_outer_shift.astype(jnp.float32)
        result, second_pull = jax.vjp(
            layer_norm,
            normed + outer_pre,
            gain_two.astype(jnp.float32),
            shift_two.astype(jnp.float32),
        )
        outputs.append(result.astype(jnp.bfloat16).reshape(local_seq, slot_count, feature_count))
        own_live = lax.dynamic_slice_in_dim(live_keys, position * local_seq, local_seq, 0)
        live_rows = own_live.astype(jnp.float32).reshape(row_count, 1)
        upstream = (
            cotangent[micro_index].reshape(row_count, feature_count).astype(jnp.float32) * live_rows
        )
        second_grad, gain_two_grad, shift_two_grad = second_pull(upstream)
        outer_low = second_grad.astype(jnp.bfloat16)
        outer_term = jnp.einsum(
            "rf,rd->fd", active_low, outer_low, preferred_element_type=jnp.float32
        )
        outer_shift_term = jnp.sum(outer_low.astype(jnp.float32), axis=0)
        (inner_grad,) = gelu_pull(
            jnp.einsum("rd,fd->rf", outer_low, full_outer, preferred_element_type=jnp.float32)
        )
        inner_low = inner_grad.astype(jnp.bfloat16)
        inner_term = jnp.einsum(
            "rd,rf->df", normed_low, inner_low, preferred_element_type=jnp.float32
        )
        inner_shift_term = jnp.sum(inner_low.astype(jnp.float32), axis=0)
        normed_grad = second_grad + jnp.einsum(
            "rf,df->rd", inner_low, full_inner, preferred_element_type=jnp.float32
        )
        first_grad, gain_one_grad, shift_one_grad = first_pull(normed_grad)
        attended_low = first_grad.astype(jnp.bfloat16)
        proj_term = jnp.einsum(
            "re,rd->ed", context_rows, attended_low, preferred_element_type=jnp.float32
        )
        proj_shift_term = jnp.sum(attended_low.astype(jnp.float32), axis=0)
        context_back = jnp.einsum(
            "rd,ed->re", attended_low, full_proj, preferred_element_type=jnp.float32
        )
        context_back = context_back.astype(jnp.bfloat16).reshape(
            local_seq, slot_count, feature_count
        )
        context_grad = lax.all_to_all(context_back, "head", split_axis=2, concat_axis=0, tiled=True)
        context_grad = context_grad.reshape(full_seq, SLOTS, local_heads, DH)
        scores_again = attention_scores(queries, keyset, live_keys)
        soft_exact = jnp.exp(scores_again - log_total)
        soft_grad = jnp.einsum(
            "sqhd,skhd->shqk", context_grad, values, preferred_element_type=jnp.float32
        )
        score_low = (
            soft_exact * (soft_grad - jnp.sum(soft_exact * soft_grad, axis=-1, keepdims=True))
        ).astype(jnp.bfloat16)
        query_grad = (
            jnp.einsum("shqk,skhd->sqhd", score_low, keyset, preferred_element_type=jnp.float32)
            * DH ** (-0.5)
        ).astype(jnp.bfloat16)
        key_grad = (
            jnp.einsum("shqk,sqhd->skhd", score_low, queries, preferred_element_type=jnp.float32)
            * DH ** (-0.5)
        ).astype(jnp.bfloat16)
        value_grad = jnp.einsum(
            "shqk,sqhd->skhd", soft_low, context_grad, preferred_element_type=jnp.float32
        ).astype(jnp.bfloat16)
        packed_grad = jnp.stack([query_grad, key_grad, value_grad], axis=3).reshape(
            full_seq * SLOTS, local_heads * 3 * DH
        )
        qkv_term = jnp.einsum(
            "nd,ne->de", token_rows, packed_grad, preferred_element_type=jnp.float32
        )
        shift_term = jnp.concatenate(
            [
                jnp.sum(query_grad.astype(jnp.float32), axis=(0, 1)),
                jnp.sum(value_grad.astype(jnp.float32), axis=(0, 1)),
            ],
            axis=1,
        )
        input_term = jnp.einsum(
            "ne,de->nd", packed_grad, local_qkv, preferred_element_type=jnp.float32
        )
        input_term = input_term.reshape(full_seq, SLOTS, feature_count)
        input_attn = lax.psum_scatter(
            input_term.astype(jnp.bfloat16), "head", scatter_dimension=0, tiled=True
        ).astype(jnp.float32)
        input_grads.append(
            (first_grad.reshape(local_seq, slot_count, feature_count) + input_attn).astype(
                jnp.bfloat16
            )
        )
        attn_terms = (qkv_term, shift_term)
        token_terms = (
            proj_term,
            proj_shift_term,
            gain_one_grad,
            shift_one_grad,
            inner_term,
            inner_shift_term,
            outer_term,
            outer_shift_term,
            gain_two_grad,
            shift_two_grad,
        )
        attn_part, token_part = spread_grads(attn_terms, token_terms)
        attn_total = add_terms(attn_total, attn_part)
        token_total = add_terms(token_total, token_part)
    layer_output = jnp.stack(outputs, axis=0)
    tokens_gradient = jnp.stack(input_grads, axis=0)
    return (
        layer_output,
        tokens_gradient,
        attn_total[0],
        attn_total[1],
        token_total[0],
        token_total[1],
        token_total[2],
        token_total[3],
        token_total[4],
        token_total[5],
        token_total[6],
        token_total[7],
        token_total[8],
        token_total[9],
    )


def solution(mesh):
    in_specs = (
        P(None, ("dp", "head"), None, None),
        P(None, "dp"),
        P(None, ("dp", "head"), None, None),
        P("dp", "head"),
        P("head", "dp"),
        P(("dp", "head"), None),
        P(("dp", "head")),
        P(("dp", "head")),
        P(("dp", "head")),
        P(("dp", "head"), None),
        P(("dp", "head")),
        P(("dp", "head"), None),
        P(("dp", "head")),
        P(("dp", "head")),
        P(("dp", "head")),
    )
    out_specs = (
        P(None, ("dp", "head"), None, None),
        P(None, ("dp", "head"), None, None),
        P("dp", "head"),
        P("head", "dp"),
        P(("dp", "head"), None),
        P(("dp", "head")),
        P(("dp", "head")),
        P(("dp", "head")),
        P(("dp", "head"), None),
        P(("dp", "head")),
        P(("dp", "head"), None),
        P(("dp", "head")),
        P(("dp", "head")),
        P(("dp", "head")),
    )
    return jax.shard_map(
        on_device, mesh=mesh, in_specs=in_specs, out_specs=out_specs, check_vma=False
    )
```

profile of v0, /device:TPU:0, one launch (start us, length us, event | category | flops | bytes accessed | tf_op | source)
XLA Modules:
  0.0 899.9 jit_solution(12388753313143966902)
XLA Ops:
  12.5 34.5 %all_gather.55 = bf16[768,576]{1,0:T(8,128)(2,1)S(1)} all-gather(bf16[96,576]{1,0:T(8,128)(2,1)S(1)} %copy-done.39), channel_id=1, replica_groups=mesh['dp'=8,'head'=4] {'dp'}, dimensions={0}, use_global_device_ids=true | all-gather | bytes 995328 | tf_op jit(solution)/shard_map/all_gather | solution.py:96
  47.8 20.3 %all-gather.2 = bf16[8,16,3]{1,2,0:T(4,128)(2,1)S(1)} all-gather(bf16[1,16,3]{1,2,0:T(4,128)(2,1)S(1)} %bitcast.301), channel_id=1, replica_groups=mesh['dp'=8,'head'=4] {'dp'}, dimensions={0}, use_global_device_ids=true | all-gather | bytes 864 | tf_op jit(solution)/shard_map/all_gather | solution.py:97
  108.6 42.4 %all-reduce.15 = (bf16[768]{0:T(1024)(128)(2,1)S(1)}, bf16[768]{0:T(1024)(128)(2,1)S(1)}, bf16[768]{0:T(1024)(128)(2,1)S(1)}, bf16[3072]{0:T(1024)(128)(2,1)S(1)...) all-reduce(bf16[768]{0:T(1024)(128)(2,1)S(1)} %dynamic-update-slice, ...), channel_id=1, replica_groups=mesh['dp'=8,'head'=4] {'dp','head'}, use_global_device_ids=true, to_apply=%add | all-reduce | flops 7680 | bytes 30720
  157.8 36.7 %all-gather.11.cloned.1.call-done = bf16[768,3072]{1,0:T(8,128)(2,1)} async-done(((bf16[24,3072]{1,0:T(8,128)(2,1)}), bf16[768,3072]{1,0:T(8,128)(2,1)}) %all-gather.11.cloned.1.call-update) | async-done | bytes 4718608 | tf_op jit(solution)/shard_map/all_gather | solution.py:115
  194.5 4.8 fusion.93
  201.9 35.0 %multiply_convert_fusion.3 = (bf16[512,3072]{1,0:T(8,128)(2,1)}, f32[512,3072]{1,0:T(8,128)}, bf16[512,3072]{1,0:T(8,128)(2,1)}, f32[512,3072]{1,0:T(8,128)}, f32[512,3072]{1,0:T(8,128)}) fusion(f32[3072]{0:T(1024)S(1)} %convert_element_type.269, f32[512,3072]{1,0:T(8,128)S(1)} %fusion.93, bf16[768,3072]{1,0:T(8,128)(2,1)S(1)} %copy-done.56, ...), kind=kOutput, calls=%fused_computation.35 | convolution fusion | flops 2625503232 | bytes 37771264 | tf_op jit(solution)/shard_map/dot_general | solution.py:154
  236.9 22.8 %all-gather.13.cloned.1.call-done = bf16[3072,768]{1,0:T(8,128)(2,1)} async-done(((bf16[96,768]{1,0:T(8,128)(2,1)}), bf16[3072,768]{1,0:T(8,128)(2,1)}) %all-gather.13.cloned.1.call-update) | async-done | bytes 4718608 | tf_op jit(solution)/shard_map/all_gather | solution.py:117
  259.7 6.2 fusion.110
  281.3 18.6 %convert_reduce_fusion.1 = (f32[3072]{0:T(1024)}, bf16[512,3072]{1,0:T(8,128)(2,1)}, f32[3072]{0:T(1024)}, bf16[512,3072]{1,0:T(8,128)(2,1)}) fusion(f32[512,3072]{1,0:T(8,128)} %get-tuple-element.63, f32[512,3072]{1,0:T(8,128)} %get-tuple-element.94, f32[3072]{0:T(1024)S(1)} %convert_element_type.269, f32[512,3072]{1,0:T(8,128)} %fusion.111, ...), kind=kOutput, calls=%fused_computation.19 | convolution fusion | flops 2469390336 | bytes 43290624 | tf_op jit(solution)/shard_map/rd,fd->rf/dot_general | solution.py:181
  299.9 6.1 add_add_fusion.6
  306.0 5.8 multiply_reduce_fusion.3
  318.8 5.4 reduce.9
  325.4 14.1 %all_to_all.80 = bf16[4,2,49152]{2,1,0:T(2,128)(2,1)S(1)} all-to-all(bf16[4,2,49152]{2,1,0:T(2,128)(2,1)S(1)} %reshape.356), channel_id=1, replica_groups=mesh['dp'=8,'head'=4] {'head'}, dimensions={0} | all-to-all | bytes 1572864 | tf_op jit(solution)/shard_map/all_to_all | solution.py:203
  340.6 8.2 multiply_reduce_fusion.1
  348.7 7.7 bitcast_reduce_fusion.2
  356.4 4.6 multiply_convert_fusion.1
  366.4 5.3 fusion.48
  382.9 5.0 copy.117
  387.9 7.3 reduce.8
  397.6 23.8 %all_to_all.81 = bf16[4,2,49152]{2,1,0:T(2,128)(2,1)} all-to-all(bf16[4,2,49152]{2,1,0:T(2,128)(2,1)} %reshape.354), channel_id=1, replica_groups=mesh['dp'=8,'head'=4] {'head'}, dimensions={0} | all-to-all | bytes 1572864 | tf_op jit(solution)/shard_map/all_to_all | solution.py:203
  426.9 11.6 %multiply_reduce_fusion = (f32[4,3,512]{2,1,0:T(4,128)S(1)}, f32[4,3,512,512]{2,3,1,0:T(8,128)}) fusion(f32[4,3,512,512]{2,3,1,0:T(8,128)} %copy-done, f32[4,3,512]{2,1,0:T(4,128)S(1)} %copy-done.32, pred[4,512]{1,0:T(4,128)(4,1)S(1)} %copy-done.36, bf16[4,512,3,64]{1,3,2,0:T(8,128)(2,1)S(1)} %bitcast.277, f32[4,512,3,3,64]{1,4,3,2,0:T(8,128)} %copy-done.3, ...), kind=kOutput, calls=%fused_computation.1 | convolution fusion | flops 419162112 | bytes 27577088 | tf_op jit(solution)/shard_map/sqhd,skhd->shqk/dot_general | solution.py:207
  439.9 7.5 multiply_convert_fusion
  467.9 5.6 fusion.113
  473.5 5.3 convolution_add_fusion
  479.5 5.5 fusion.95
  485.0 5.8 convolution_add_fusion.1
  491.6 5.3 all-to-all-start.7
  513.5 4.7 all-to-all-start.4
  527.4 13.5 %all-to-all-done.4 = bf16[8,96,576]{2,1,0:T(8,128)(2,1)S(1)} async-done(((bf16[8,96,576]{2,1,0:T(8,128)(2,1)}), bf16[8,96,576]{2,1,0:T(8,128)(2,1)S(1)}, u32[]{:S(2)}, u32[]{:S(2)}) %all-to-all-start.4) | async-done | bytes 884768 | tf_op jit(solution)/shard_map/all_to_all | solution.py:20
  545.3 49.0 %all-reduce.14 = (f32[768]{0:T(1024)S(1)}, f32[768]{0:T(1024)S(1)}, f32[768]{0:T(1024)S(1)}, f32[3072]{0:T(1024)S(1)}, f32[768]{0:T(1024)S(1)}, /*index=5*/f32[768]{0:T(1024)S(1)}, f32[768]{0:T(1024)S(1)}) all-reduce(f32[768]{0:T(1024)S(1)} %add.311, f32[768]{0:T(1024)S(1)} %add.312, ...), channel_id=17, replica_groups=mesh['dp'=8,'head'=4] {'dp','head'}, use_global_device_ids=true, to_apply=%region_35.36.clone | all-reduce | flops 7680 | bytes 61440
  609.6 142.2 %reduce-scatter.14.cloned.1.call-done = f32[96,768]{1,0:T(8,128)} async-done(((f32[3072,768]{1,0:T(8,128)}), f32[96,768]{1,0:T(8,128)}) %reduce-scatter.14.cloned.1.call-update) | async-done | bytes 294928 | tf_op jit(solution)/shard_map/reduce_scatter | solution.py:53
  751.7 140.9 %reduce-scatter.12.cloned.1.call-done = f32[24,3072]{1,0:T(8,128)} async-done(((f32[768,3072]{1,0:T(8,128)}), f32[24,3072]{1,0:T(8,128)}) %reduce-scatter.12.cloned.1.call-update) | async-done | bytes 294928 | tf_op jit(solution)/shard_map/reduce_scatter | solution.py:51
  (327 shorter events, 172.4 us)
Async XLA Ops:
  7.2 61.2 %all-gather.15.cloned.1.call-start = ((), (), s32[]{:S(2)}) async-start(), calls=%async_computation.18 | async-start | bytes 3932160 | tf_op jit(solution)/shard_map/all_gather | solution.py:123
  9.8 37.8 %copy-start.55 = (s32[2,4]{1,0:T(2,128)S(1)}, s32[2,4]{1,0:T(2,128)}, u32[]{:S(2)}) copy-start(s32[2,4]{1,0:T(2,128)} %param.16) | copy-start | bytes 100
  9.8 37.9 %copy-start.54 = (bf16[3,16]{1,0:T(4,128)(2,1)S(1)}, bf16[3,16]{1,0:T(4,128)(2,1)}, u32[]{:S(2)}) copy-start(bf16[3,16]{1,0:T(4,128)(2,1)} %param.19) | copy-start | bytes 292
  9.9 77.5 %all-gather.17.cloned.1.call-start = ((), (), s32[]{:S(2)}) async-start(), calls=%async_computation.19 | async-start | bytes 3932160 | tf_op jit(solution)/shard_map/all_gather | solution.py:123
  10.6 140.5 %all-gather.9.cloned.1.call-start = ((), (), s32[]{:S(2)}) async-start(), calls=%async_computation.13 | async-start | bytes 1216512 | tf_op jit(solution)/shard_map/all_gather | solution.py:111
  11.4 183.1 %all-gather.11.cloned.1.call-start = ((), (), s32[]{:S(2)}) async-start(), calls=%async_computation.14 | async-start | bytes 4866048 | tf_op jit(solution)/shard_map/all_gather | solution.py:115
  11.9 247.7 %all-gather.13.cloned.1.call-start = ((), (), s32[]{:S(2)}) async-start(), calls=%async_computation.15 | async-start | bytes 4866048 | tf_op jit(solution)/shard_map/all_gather | solution.py:117
  47.1 25.3 %copy-start.16 = (bf16[768,576]{1,0:T(8,128)(2,1)}, bf16[768,576]{1,0:T(8,128)(2,1)S(1)}, u32[]{:S(2)}) copy-start(bf16[768,576]{1,0:T(8,128)(2,1)S(1)} %all_gather.55) | copy-start | bytes 2654212
  47.8 31.2 %copy-start.37 = (pred[4,512]{1,0:T(4,128)(4,1)}, pred[4,512]{1,0:T(4,128)(4,1)S(1)}, u32[]{:S(2)}) copy-start(pred[4,512]{1,0:T(4,128)(4,1)S(1)} %iota_compare_fusion.1) | copy-start | bytes 6148
  68.3 29.6 %copy-start.44 = (f32[3,64]{1,0:T(4,128)}, f32[3,64]{1,0:T(4,128)S(1)}, u32[]{:S(2)}) copy-start(f32[3,64]{1,0:T(4,128)S(1)} %get-tuple-element.83) | copy-start | bytes 2308
  68.3 38.6 %copy-start.35 = (pred[4,512]{1,0:T(4,128)(4,1)}, pred[4,512]{1,0:T(4,128)(4,1)S(1)}, u32[]{:S(2)}) copy-start(pred[4,512]{1,0:T(4,128)(4,1)S(1)} %iota_compare_fusion) | copy-start | bytes 6148
  83.6 19.7 %all-to-all-start = ((bf16[4,512,192]{1,2,0:T(8,128)(2,1)}), bf16[4,512,192]{1,2,0:T(8,128)(2,1)S(1)}, u32[]{:S(2)}, u32[]{:S(2)}) async-start(bf16[4,512,192]{1,2,0:T(8,128)(2,1)} %bitcast.15), calls=%async_computation | async-start | bytes 1572864 | tf_op jit(solution)/shard_map/all_to_all | solution.py:141
  103.3 50.2 %copy-start.27 = (bf16[4,512,192]{1,2,0:T(8,128)(2,1)}, bf16[4,512,192]{1,2,0:T(8,128)(2,1)S(1)}, u32[]{:S(2)}) copy-start(bf16[4,512,192]{1,2,0:T(8,128)(2,1)S(1)} %all-to-all-done) | copy-start | bytes 2359300
  103.3 50.2 %all-to-all-start.1 = ((bf16[4,512,192]{1,2,0:T(8,128)(2,1)}), bf16[4,512,192]{1,2,0:T(8,128)(2,1)S(1)}, u32[]{:S(2)}, u32[]{:S(2)}) async-start(bf16[4,512,192]{1,2,0:T(8,128)(2,1)} %bitcast.30), calls=%async_computation.1 | async-start | bytes 1572864 | tf_op jit(solution)/shard_map/all_to_all | solution.py:141
  106.8 495.9 %reduce-scatter.6.cloned.1.call-start = ((), (), s32[]{:S(2)}) async-start(), calls=%async_computation.16 | async-start | bytes 3932160 | tf_op jit(solution)/shard_map/reduce_scatter | solution.py:241
  151.0 115.2 %copy-start.40 = (f32[768]{0:T(1024)}, f32[768]{0:T(1024)S(1)}, u32[]{:S(2)}) copy-start(f32[768]{0:T(1024)S(1)} %convert_element_type.267) | copy-start | bytes 9220
  153.5 112.7 %copy-start.14 = (f32[512,768]{1,0:T(8,128)}, f32[512,768]{1,0:T(8,128)S(1)}, u32[]{:S(2)}) copy-start(f32[512,768]{1,0:T(8,128)S(1)} %get-tuple-element.89) | copy-start | bytes 4718596
  157.1 154.7 %copy-start.7 = (f32[512,768]{1,0:T(8,128)}, f32[512,768]{1,0:T(8,128)S(1)}, u32[]{:S(2)}) copy-start(f32[512,768]{1,0:T(8,128)S(1)} %get-tuple-element.93) | copy-start | bytes 4718596
  377.3 227.6 %reduce-scatter.8.cloned.1.call-start = ((), (), s32[]{:S(2)}) async-start(), calls=%async_computation.17 | async-start | bytes 3932160 | tf_op jit(solution)/shard_map/reduce_scatter | solution.py:241
  397.6 29.3 %copy-start.32 = (f32[4,3,512]{2,1,0:T(4,128)S(1)}, f32[4,3,512]{2,1,0:T(4,128)}, u32[]{:S(2)}) copy-start(f32[4,3,512]{2,1,0:T(4,128)} %copy-done.31) | copy-start | bytes 73732
  397.6 29.3 %copy-start.36 = (pred[4,512]{1,0:T(4,128)(4,1)S(1)}, pred[4,512]{1,0:T(4,128)(4,1)}, u32[]{:S(2)}) copy-start(pred[4,512]{1,0:T(4,128)(4,1)} %copy-done.35) | copy-start | bytes 6148
  421.4 26.0 %slice-start.6 = ((s8[4718592]{0:T(1024)(128)(4,1)}), s8[524288]{0:T(1024)(128)(4,1)S(1)}, s32[]{:S(2)}) async-start(s8[4718592]{0:T(1024)(128)(4,1)} %bitcast.269), calls=%async_computation.29 | async-start | bytes 1048576
  461.7 147.8 %reduce-scatter.10.cloned.1.call-start = ((), (), s32[]{:S(2)}) async-start(), calls=%async_computation.20 | async-start | bytes 2433024 | tf_op jit(solution)/shard_map/reduce_scatter | solution.py:47
  467.6 284.2 %reduce-scatter.14.cloned.1.call-start = ((), (), s32[]{:S(2)}) async-start(), calls=%async_computation.22 | async-start | bytes 9732096 | tf_op jit(solution)/shard_map/reduce_scatter | solution.py:53
  478.9 413.8 %reduce-scatter.12.cloned.1.call-start = ((), (), s32[]{:S(2)}) async-start(), calls=%async_computation.21 | async-start | bytes 9732096 | tf_op jit(solution)/shard_map/reduce_scatter | solution.py:51
  491.6 11.9 %all-to-all-start.7 = ((bf16[8,3,16]{2,1,0:T(4,128)(2,1)}), bf16[8,3,16]{2,1,0:T(4,128)(2,1)S(1)}, u32[]{:S(2)}, u32[]{:S(2)}) async-start(bf16[8,3,16]{2,1,0:T(4,128)(2,1)} %copy.127), calls=%async_computation.9 | async-start | bytes 16384 | tf_op jit(solution)/shard_map/all_to_all | solution.py:20
  503.5 10.0 %all-to-all-start.6 = ((bf16[8,3,16]{2,1,0:T(4,128)(2,1)}), bf16[8,3,16]{2,1,0:T(4,128)(2,1)S(1)}, u32[]{:S(2)}, u32[]{:S(2)}) async-start(bf16[8,3,16]{2,1,0:T(4,128)(2,1)} %copy.126), calls=%async_computation.8 | async-start | bytes 16384 | tf_op jit(solution)/shard_map/all_to_all | solution.py:20
  513.5 27.4 %all-to-all-start.4 = ((bf16[8,96,576]{2,1,0:T(8,128)(2,1)}), bf16[8,96,576]{2,1,0:T(8,128)(2,1)S(1)}, u32[]{:S(2)}, u32[]{:S(2)}) async-start(bf16[8,96,576]{2,1,0:T(8,128)(2,1)} %bitcast.68), calls=%async_computation.6 | async-start | bytes 1966080 | tf_op jit(solution)/shard_map/all_to_all | solution.py:20
  525.0 73.4 %copy-start.23 = (bf16[1,1,512,768]{3,2,1,0:T(8,128)(2,1)S(1)}, bf16[1,1,512,768]{3,2,1,0:T(8,128)(2,1)}, u32[]{:S(2)}) copy-start(bf16[1,1,512,768]{3,2,1,0:T(8,128)(2,1)} %get-tuple-element.67) | copy-start | bytes 2359300
  525.0 73.4 %copy-start.24 = (bf16[1,1,512,768]{3,2,1,0:T(8,128)(2,1)S(1)}, bf16[1,1,512,768]{3,2,1,0:T(8,128)(2,1)}, u32[]{:S(2)}) copy-start(bf16[1,1,512,768]{3,2,1,0:T(8,128)(2,1)} %get-tuple-element.68) | copy-start | bytes 2359300
  540.9 57.5 %copy-start.19 = (bf16[8,96,576]{2,1,0:T(8,128)(2,1)}, bf16[8,96,576]{2,1,0:T(8,128)(2,1)S(1)}, u32[]{:S(2)}) copy-start(bf16[8,96,576]{2,1,0:T(8,128)(2,1)S(1)} %all-to-all-done.4) | copy-start | bytes 2654212
  540.9 59.6 %all-to-all-start.5 = ((bf16[8,96,576]{2,1,0:T(8,128)(2,1)}), bf16[8,96,576]{2,1,0:T(8,128)(2,1)}, u32[]{:S(2)}, u32[]{:S(2)}) async-start(bf16[8,96,576]{2,1,0:T(8,128)(2,1)} %bitcast.71), calls=%async_computation.7 | async-start | bytes 1966080 | tf_op jit(solution)/shard_map/all_to_all | solution.py:20
  (62 other events, 522.2 us)
Sparse Core Ops, SparseCore 0:
  10.2 31.2 all-gather.14
  43.6 28.5 all-gather.16
  75.0 54.0 all-gather.8
  131.9 62.5 all-gather.10
  197.2 62.4 all-gather.12
  377.5 44.5 reduce-scatter.5
  461.8 37.7 reduce-scatter.7
  505.5 104.0 reduce-scatter.9
  617.0 134.6 reduce-scatter.13
  758.1 134.5 reduce-scatter.11
where the time goes:
time: 908 us; the launch traced here: 900 us
  waiting for transfers between devices  365 us (40%)
  matrix products  200 us (22%)
  blocking collectives  184 us (20%)
  local copies, waits for them, and re-layouts  54.8 us (6%)
  other arithmetic  54.6 us (6%)
  starting transfers between devices  25.7 us (3%)
  between operations  15.9 us (2%)
    reduce_scatter x1, waiting for transfers between devices, spread_grads(): lax.psum_scatter(token_terms[6], ('dp', 'head'), scatter_dimension=0, til...  142 us
    reduce_scatter x1, waiting for transfers between devices, spread_grads(): lax.psum_scatter(token_terms[4], ('dp', 'head'), scatter_dimension=0, til...  141 us
    unnamed x2, blocking collectives  91.4 us
    dot_general x2, matrix products, on_device(): jnp.dot(normed_low, full_inner, preferred_element_type=jnp.float32)  39.8 us
    all_to_all x2, blocking collectives, on_device(): lax.all_to_all(context_back, 'head', split_axis=2, concat_axis=0, tiled=T...  38 us
    all_gather x1, waiting for transfers between devices, on_device(): lax.all_gather(inner_weight, ('dp', 'head'), axis=0, tiled=True)  36.7 us
    unnamed x186, local copies, waits for them, and re-layouts  35.8 us
    all_gather x1, blocking collectives, on_device(): lax.all_gather(qkv_weight, 'dp', axis=0, tiled=True)  34.5 us
  transfers between devices with their start and end apart: 16, of which 8 were waited for; matrix products, arithmetic and copies ran while one was open for 21% of the time, Pallas kernels for 0%

commit v1 on v0

v1 whole, which is shorter than its diff:
```python
import jax
import jax.numpy as jnp
from jax import lax
from jax.experimental import pallas as pl
from jax.experimental.pallas import tpu as pltpu
from jax.sharding import PartitionSpec as P

DH = 64
EPSILON = 1e-12
AXES = ("dp", "head")
LOW = jnp.bfloat16
F32 = jnp.float32


def flat(z, y, x, c):
    return ((z * 2 + y) * 2 + x) * 2 + c


def move(value, dz=0, dy=0, dx=0, dc=0):
    pairs = [
        (flat(z, y, x, c), flat((z + dz) % 4, y ^ dy, x ^ dx, c ^ dc))
        for z in range(4)
        for y in range(2)
        for x in range(2)
        for c in range(2)
    ]
    return lax.ppermute(value, AXES, pairs)


def coords():
    dp, head = lax.axis_index("dp"), lax.axis_index("head")
    return jnp.stack([dp // 2, dp % 2, head // 2, head % 2]).astype(jnp.int32)


PIECES = [
    (ry, rx, rc, first, count)
    for rc in (0, 1)
    for ry, rx, first, count in ((0, 0, 0, 4), (1, 0, 0, 4), (0, 1, 0, 4), (1, 1, 0, 2), (1, 1, 2, 2))
]


def gather_pieces(shard):
    own = shard[None]
    plane = jnp.concatenate([own] + [move(own, dz=k) for k in (1, 2, 3)], axis=0)
    from_y = move(plane, dy=1)
    from_x = move(plane, dx=1)
    far_a = move(from_y[:2], dx=1)
    far_b = move(from_x[2:], dy=1)
    mine = [plane, from_y, from_x, far_a, far_b]
    return mine + [move(piece, dc=1) for piece in mine]


def assemble(shard, where):
    pieces = gather_pieces(shard)

    def body(where_ref, *refs):
        ins, out, sems = refs[: len(PIECES)], refs[len(PIECES)], refs[len(PIECES) + 1]
        z, y, x, c = (where_ref[i] for i in range(4))
        copies = []
        for ref, (ry, rx, rc, first, count) in zip(ins, PIECES):
            for k in range(count):
                source_z = lax.rem(z + 4 - (first + k), 4)
                target = flat(source_z, y ^ ry, x ^ rx, c ^ rc)
                copy = pltpu.make_async_copy(ref.at[k], out.at[target], sems.at[len(copies)])
                copy.start()
                copies.append(copy)
        for copy in copies:
            copy.wait()

    return pl.pallas_call(
        body,
        out_shape=jax.ShapeDtypeStruct((32,) + shard.shape, shard.dtype),
        in_specs=[pl.BlockSpec(memory_space=pltpu.SMEM)] + [pl.BlockSpec(memory_space=pl.ANY)] * len(pieces),
        out_specs=pl.BlockSpec(memory_space=pl.ANY),
        scratch_shapes=[pltpu.SemaphoreType.DMA((32,))],
        name="assemble",
    )(where, *pieces)


def split_parts(full, where):
    def body(where_ref, full_ref, keep_ref, send_ref, sems):
        z, y, x, c = (where_ref[i] for i in range(4))
        copies = []
        for rc, out in ((0, keep_ref), (1, send_ref)):
            for ry in (0, 1):
                for rx in (0, 1):
                    for rz in range(4):
                        source = flat(lax.rem(z + rz, 4), y ^ ry, x ^ rx, c ^ rc)
                        copy = pltpu.make_async_copy(full_ref.at[source], out.at[ry, rx, rz], sems.at[len(copies)])
                        copy.start()
                        copies.append(copy)
        for copy in copies:
            copy.wait()

    half = jax.ShapeDtypeStruct((2, 2, 4) + full.shape[1:], full.dtype)
    return pl.pallas_call(
        body,
        out_shape=(half, half),
        in_specs=[pl.BlockSpec(memory_space=pltpu.SMEM), pl.BlockSpec(memory_space=pl.ANY)],
        out_specs=(pl.BlockSpec(memory_space=pl.ANY), pl.BlockSpec(memory_space=pl.ANY)),
        scratch_shapes=[pltpu.SemaphoreType.DMA((32,))],
        name="split_parts",
    )(where, full)


def reduce_parts(kept, sent):
    kind = kept.dtype

    def add(first, *rest):
        total = first.astype(F32)
        for term in rest:
            total = total + term.astype(F32)
        return total

    here = add(kept, move(sent, dc=1)).astype(kind)
    far = here[1, 1]
    near_y, near_x = here[1, 0], here[0, 1]
    via_x = move(far[:2], dx=1)
    via_y = move(far[2:], dy=1)
    to_y = jnp.concatenate([add(near_y[:2], via_x).astype(kind), near_y[2:]], axis=0)
    to_x = jnp.concatenate([near_x[:2], add(near_x[2:], via_y).astype(kind)], axis=0)
    plane = add(here[0, 0], move(to_y, dy=1), move(to_x, dx=1))
    low = plane.astype(kind)
    return add(plane[0], *[move(low[k], dz=k) for k in (1, 2, 3)])


def norm_stats(hidden):
    center = hidden - jnp.mean(hidden, axis=-1, keepdims=True)
    spread = jnp.mean(center * center, axis=-1, keepdims=True)
    inverse = lax.rsqrt(spread + EPSILON)
    return center * inverse, inverse


def norm_back(grad_hat, hat, inverse):
    return inverse * (
        grad_hat
        - jnp.mean(grad_hat, axis=-1, keepdims=True)
        - hat * jnp.mean(grad_hat * hat, axis=-1, keepdims=True)
    )


def gelu_both(values):
    half = 0.5 * (1.0 + lax.erf(values * 0.7071067811865476))
    slope = half + values * jnp.exp(-0.5 * values * values) * 0.3989422804014327
    return values * half, slope


def mm(a, b, dims):
    return lax.dot_general(a, b, (dims, ((), ())), preferred_element_type=F32)


def layer(tokens, lengths, cotangent, weights):
    qkv, qv_shift, proj, proj_shift, gain_one, shift_one, inner, inner_shift, outer, outer_shift, gain_two, shift_two = weights
    rows, slots, features = tokens.shape
    groups, _, width = qkv.shape
    per = width // (3 * DH)
    heads = groups * per
    count = rows * slots
    live = jnp.arange(slots, dtype=jnp.int32)[None, :] < lengths[:, None]
    packed = jnp.einsum("bsd,gde->bsge", tokens, qkv, preferred_element_type=F32)
    packed = packed.reshape(rows, slots, heads, 3, DH)
    queries = (packed[:, :, :, 0] + qv_shift[:, :DH]).astype(LOW)
    keyset = packed[:, :, :, 1].astype(LOW)
    values = (packed[:, :, :, 2] + qv_shift[:, DH:]).astype(LOW)

    def scored(q, k):
        scores = jnp.einsum("bqhd,bkhd->bhqk", q, k, preferred_element_type=F32) * DH**-0.5
        return jnp.where(live[:, None, None, :], scores, -1e30)

    scores = scored(queries, keyset)
    highest = jnp.max(scores, axis=-1, keepdims=True)
    raised = jnp.exp(scores - highest)
    soft_low = (raised / jnp.sum(raised, axis=-1, keepdims=True)).astype(LOW)
    context = jnp.einsum("bhqk,bkhd->bqhd", soft_low, values, preferred_element_type=F32)
    context = context.astype(LOW).reshape(count, features)
    flat_tokens = tokens.reshape(count, features)
    first = flat_tokens.astype(F32) + mm(context, proj, ((1,), (0,))) + proj_shift
    hat_one, inverse_one = norm_stats(first)
    normed = hat_one * gain_one + shift_one
    normed_low = normed.astype(LOW)
    active, slope = gelu_both(mm(normed_low, inner, ((1,), (0,))) + inner_shift)
    active_low = active.astype(LOW)
    second = normed + mm(active_low, outer, ((1,), (0,))) + outer_shift
    hat_two, inverse_two = norm_stats(second)
    result = (hat_two * gain_two + shift_two).astype(LOW).reshape(tokens.shape)
    upstream = cotangent.reshape(count, features).astype(F32) * live.reshape(count, 1).astype(F32)
    gain_two_grad = jnp.sum(upstream * hat_two, axis=0)
    shift_two_grad = jnp.sum(upstream, axis=0)
    second_grad = norm_back(upstream * gain_two, hat_two, inverse_two)
    outer_low = second_grad.astype(LOW)
    outer_grad = mm(active_low, outer_low, ((0,), (0,))).astype(LOW)
    outer_shift_grad = jnp.sum(outer_low.astype(F32), axis=0)
    inner_low = (mm(outer_low, outer, ((1,), (1,))) * slope).astype(LOW)
    inner_grad = mm(normed_low, inner_low, ((0,), (0,))).astype(LOW)
    inner_shift_grad = jnp.sum(inner_low.astype(F32), axis=0)
    normed_grad = second_grad + mm(inner_low, inner, ((1,), (1,)))
    gain_one_grad = jnp.sum(normed_grad * hat_one, axis=0)
    shift_one_grad = jnp.sum(normed_grad, axis=0)
    first_grad = norm_back(normed_grad * gain_one, hat_one, inverse_one)
    attended_low = first_grad.astype(LOW)
    proj_grad = mm(context, attended_low, ((0,), (0,))).astype(LOW)
    proj_shift_grad = jnp.sum(attended_low.astype(F32), axis=0)
    context_grad = mm(attended_low, proj, ((1,), (1,))).astype(LOW).reshape(rows, slots, heads, DH)
    soft = soft_low.astype(F32)
    soft_grad = jnp.einsum("bqhd,bkhd->bhqk", context_grad, values, preferred_element_type=F32)
    score_low = (soft * (soft_grad - jnp.sum(soft * soft_grad, axis=-1, keepdims=True))).astype(LOW)
    query_grad = jnp.einsum("bhqk,bkhd->bqhd", score_low, keyset, preferred_element_type=F32) * DH**-0.5
    key_grad = jnp.einsum("bhqk,bqhd->bkhd", score_low, queries, preferred_element_type=F32) * DH**-0.5
    value_grad = jnp.einsum("bhqk,bqhd->bkhd", soft_low, context_grad, preferred_element_type=F32)
    packed_grad = jnp.stack([query_grad, key_grad, value_grad], axis=3).astype(LOW)
    shift_grad = jnp.sum(packed_grad.astype(F32), axis=(0, 1))
    qv_shift_grad = jnp.concatenate([shift_grad[:, 0], shift_grad[:, 2]], axis=1)
    packed_grad = packed_grad.reshape(count, groups, width)
    qkv_grad = jnp.einsum("nd,nge->gde", flat_tokens, packed_grad, preferred_element_type=F32).astype(LOW)
    input_grad = first_grad + jnp.einsum("nge,gde->nd", packed_grad, qkv, preferred_element_type=F32)
    input_grad = input_grad.astype(LOW).reshape(tokens.shape)
    grads = (
        qkv_grad, qv_shift_grad, proj_grad, proj_shift_grad, gain_one_grad, shift_one_grad,
        inner_grad, inner_shift_grad, outer_grad, outer_shift_grad, gain_two_grad, shift_two_grad,
    )
    return result, input_grad, grads


def on_device(*args):
    tokens, lengths, cotangent = args[:3]
    params = args[3:]
    qkv_weight, qv_shift, proj_weight, proj_shift, first_gain, first_shift = params[:6]
    inner_weight, inner_shift, outer_weight, outer_shift, second_gain, second_shift = params[6:]
    micro, local, slots, features = tokens.shape
    dp, groups = lax.axis_size("dp"), lax.axis_size("head")
    staged = (dp, groups) == (8, 4)
    position = lax.axis_index("head")
    where = coords()
    own = lax.dynamic_slice_in_dim(lengths, position * local, local, 1).reshape(micro * local)
    rows = tokens.reshape(micro * local, slots, features)
    upstream = cotangent.reshape(micro * local, slots, features)

    vectors = [proj_shift, first_gain, first_shift, outer_shift, second_gain, second_shift, inner_shift, qv_shift.reshape(-1)]
    lens = [v.shape[0] for v in vectors]
    total = sum(lens)
    padded = -(-total // 1024) * 1024
    small = jnp.pad(jnp.concatenate(vectors), (0, padded - total)).reshape(8, padded // 8)

    def everyone(shard):
        if staged:
            return assemble(shard, where)
        return lax.all_gather(shard, AXES, axis=0)

    qkv_all = everyone(qkv_weight)
    small_all = everyone(small).reshape(dp * groups, padded)
    proj = everyone(proj_weight).reshape(-1, features)
    inner = everyone(inner_weight).reshape(features, -1)
    outer = everyone(outer_weight).reshape(-1, features)
    depth, width = qkv_weight.shape
    qkv = qkv_all.reshape(dp, groups, depth, width).swapaxes(0, 1).reshape(groups, dp * depth, width)
    pieces, at = [], 0
    for size in lens:
        pieces.append(small_all[:, at : at + size].astype(F32))
        at += size
    full = [p.reshape(-1) for p in pieces[:-1]]
    shift = pieces[-1].reshape((dp, groups) + qv_shift.shape).transpose(1, 2, 0, 3).reshape(-1, 2 * DH)
    weights = (qkv, shift, proj, full[0], full[1], full[2], inner, full[6], outer, full[3], full[4], full[5])
    result, input_grad, grads = layer(rows, own, upstream, weights)
    (
        qkv_grad, qv_shift_grad, proj_grad, proj_shift_grad, gain_one_grad, shift_one_grad,
        inner_grad, inner_shift_grad, outer_grad, outer_shift_grad, gain_two_grad, shift_two_grad,
    ) = grads

    def owner(grad):
        if staged:
            return reduce_parts(*split_parts(grad, where))
        parts = lax.all_to_all(grad, AXES, 0, 0, tiled=True)
        return jnp.sum(parts.astype(F32), axis=0)

    devices = dp * groups
    outer_out = owner(outer_grad.reshape((devices,) + outer_weight.shape))
    inner_out = owner(inner_grad.reshape((devices,) + inner_weight.shape))
    proj_out = owner(proj_grad.reshape((devices,) + proj_weight.shape))
    qkv_blocks = qkv_grad.reshape(groups, dp, depth, width).swapaxes(0, 1)
    qkv_out = owner(qkv_blocks.reshape(devices, depth, width))
    shift_blocks = qv_shift_grad.reshape(groups, qv_shift.shape[0], dp, qv_shift.shape[1]).transpose(2, 0, 1, 3)
    vector_grads = [proj_shift_grad, gain_one_grad, shift_one_grad, outer_shift_grad, gain_two_grad, shift_two_grad, inner_shift_grad, shift_blocks]
    small_grad = jnp.concatenate([g.reshape(devices, -1) for g in vector_grads], axis=1)
    small_grad = jnp.pad(small_grad, ((0, 0), (0, padded - total))).reshape(devices, 8, padded // 8)
    small_out = owner(small_grad).reshape(padded)
    outs, at = [], 0
    for size in lens:
        outs.append(small_out[at : at + size])
        at += size
    return (
        result.reshape(tokens.shape), input_grad.reshape(tokens.shape),
        qkv_out, outs[7].reshape(qv_shift.shape), proj_out, outs[0], outs[1], outs[2],
        inner_out, outs[6], outer_out, outs[3], outs[4], outs[5],
    )


def solution(mesh):
    both = ("dp", "head")
    rows, whole = P(both), P(both, None)
    data = P(None, both, None, None)
    params = (P("dp", "head"), P("head", "dp"), whole, rows, rows, rows, whole, rows, whole, rows, rows, rows)
    in_specs = (data, P(None, "dp"), data) + params
    out_specs = (data, data) + params
    return jax.shard_map(on_device, mesh=mesh, in_specs=in_specs, out_specs=out_specs, check_vma=False)
```

time: 908 us -> 1390 us (1.53)
  Pallas kernels: 0 us -> 908 us
  waiting for transfers between devices: 365 us -> 90.5 us
  blocking collectives: 184 us -> 0 us
  starting transfers between devices: 25.7 us -> 92.6 us
  matrix products: 200 us -> 138 us
  local copies, waits for them, and re-layouts: 54.8 us -> 90.6 us
    pallas_call x0 -> x10, Pallas kernels: none -> 908 us  [the longest x5 455 us: split_parts(): pl.pallas_call(body, out_shape=(half, half), in_specs=[pl.BlockSpec(memor...]
    reduce_scatter x5 -> x0, waiting for transfers between devices: 285 us -> none  [the longest x1 142 us: spread_grads(): lax.psum_scatter(token_terms[6], ('dp', 'head'), scatter_dimension=0, til...]
    ppermute x0 -> x100, starting transfers between devices: none -> 92.6 us  [move(): return lax.ppermute(value, AXES, pairs)]
    unnamed x2 -> x0, blocking collectives: 91.4 us -> none
    ppermute x0 -> x100, waiting for transfers between devices: none -> 90.5 us  [move(): return lax.ppermute(value, AXES, pairs)]
    dot_general x36 -> x17, matrix products: 200 us -> 120 us  [the longest x9 61.4 us: mm(): return lax.dot_general(a, b, (dims, ((), ())), preferred_element_type=F32)]
    all_gather x5 -> x0, waiting for transfers between devices: 59.6 us -> none  [the longest x1 36.7 us: on_device(): lax.all_gather(inner_weight, ('dp', 'head'), axis=0, tiled=True)]
    all_gather x2 -> x0, blocking collectives: 54.8 us -> none  [the longest x1 34.5 us: on_device(): lax.all_gather(qkv_weight, 'dp', axis=0, tiled=True)]
  transfers between devices with their start and end apart: 16 -> 100, of which waited for: 8 -> 28; matrix products, arithmetic and copies ran while one was open for 21% -> 11% of each run, Pallas kernels for 0% -> 55%
where the time goes in v1:
time: 1390 us; the launch traced here: 1380 us
  Pallas kernels  908 us (65%)
  matrix products  138 us (10%)
  starting transfers between devices  92.6 us (7%)
  local copies, waits for them, and re-layouts  90.6 us (7%)
  waiting for transfers between devices  90.5 us (7%)
  other arithmetic  59.9 us (4%)
    pallas_call x5, Pallas kernels, split_parts(): pl.pallas_call(body, out_shape=(half, half), in_specs=[pl.BlockSpec(memor...  455 us
    pallas_call x5, Pallas kernels, assemble(): pl.pallas_call(body, out_shape=jax.ShapeDtypeStruct((32,) + shard.shape,...  453 us
    ppermute x100, starting transfers between devices, move(): return lax.ppermute(value, AXES, pairs)  92.6 us
    ppermute x100, waiting for transfers between devices, move(): return lax.ppermute(value, AXES, pairs)  90.5 us
    dot_general x9, matrix products, mm(): return lax.dot_general(a, b, (dims, ((), ())), preferred_element_type=F32)  61.4 us
  transfers between devices with their start and end apart: 100, of which 28 were waited for; matrix products, arithmetic and copies ran while one was open for 11% of the time, Pallas kernels for 55%

profile of v1, /device:TPU:0, one launch (start us, length us, event | category | flops | bytes accessed | tf_op | source)
XLA Modules:
  0.0 1382.0 jit_solution(5486884665815178802)
XLA Ops:
  34.3 7.8 collective-permute-done
  49.4 8.4 collective-permute-start.38
  89.4 6.0 collective-permute-done.4.refs_2_
  113.8 7.0 collective-permute-done.52.refs_2_
  126.1 37.8 %assemble.7 = bf16[32,24,768]{2,1,0:T(8,128)(2,1)} custom-call(s32[4]{0:T(128)} %pad_add_fusion.where_ref, bf16[4,24,768]{2,1,0:T(8,128)(2,1)} %copy-done.25, bf16[4,24,768]{2,1,0:T(8,128)(2,1)} %copy-done.27, bf16[4,24,768]{2,1,0:T(8,128)(2,1)} %collective-permute-done.28.refs_2_, bf16[2,24,768]{2,1,0:T(8,128)(2,1)} %copy-done.44, ...), custom_call_target="tpu_custom_call" | custom-call | tf_op jit(solution)/shard_map/assemble/pallas_call | solution.py:70
  173.7 121.2 %assemble.5 = bf16[32,96,576]{2,1,0:T(8,128)(2,1)} custom-call(s32[4]{0:T(128)} %pad_add_fusion.where_ref, bf16[4,96,576]{2,1,0:T(8,128)(2,1)} %copy-done.18, bf16[4,96,576]{2,1,0:T(8,128)(2,1)} %copy-done.22, bf16[4,96,576]{2,1,0:T(8,128)(2,1)} %copy-done.23, bf16[2,96,576]{2,1,0:T(8,128)(2,1)} %copy-done.35, ...), custom_call_target="tpu_custom_call" | custom-call | tf_op jit(solution)/shard_map/assemble/pallas_call | solution.py:70
  306.8 17.7 %fusion.87 = (f32[2,12,512]{2,1,0:T(8,128)S(1)}, f32[2,12,512,512]{2,3,1,0:T(8,128)}) fusion(pred[2,512]{1,0:T(4,128)(4,1)S(1)} %copy-done.66, f32[2,512,12,3,64]{1,4,3,2,0:T(8,128)} %bitcast.346, f32[12,64]{1,0:T(8,128)S(1)} %copy-done.43), kind=kOutput, calls=%fused_computation.231 | convolution fusion | flops 832045568 | bytes 29937664 | tf_op jit(solution)/shard_map/sub | solution.py:172
  324.5 10.4 divide_convert_fusion
  346.6 6.4 collective-permute-done.54.refs_4_
  355.0 145.0 %assemble.8 = bf16[32,24,3072]{2,1,0:T(8,128)(2,1)} custom-call(s32[4]{0:T(128)} %pad_add_fusion.where_ref, bf16[4,24,3072]{2,1,0:T(8,128)(2,1)} %copy-done.14, bf16[4,24,3072]{2,1,0:T(8,128)(2,1)} %collective-permute-done.39.refs_1_, bf16[4,24,3072]{2,1,0:T(8,128)(2,1)} %collective-permute-done.40.refs_2_, bf16[2,24,3072]{2,1,0:T(8,128)(2,1)} %copy-done.29, ...), custom_call_target="tpu_custom_call" | custom-call | tf_op jit(solution)/shard_map/assemble/pallas_call | solution.py:70
  500.0 12.5 multiply_convert_fusion
  512.5 145.0 %assemble.9 = bf16[32,96,768]{2,1,0:T(8,128)(2,1)} custom-call(s32[4]{0:T(128)} %pad_add_fusion.where_ref, bf16[4,96,768]{2,1,0:T(8,128)(2,1)} %copy-done.13, bf16[4,96,768]{2,1,0:T(8,128)(2,1)} %collective-permute-done.51.refs_1_, bf16[4,96,768]{2,1,0:T(8,128)(2,1)} %collective-permute-done.52.refs_2_, bf16[2,96,768]{2,1,0:T(8,128)(2,1)} %copy-done.28, ...), custom_call_target="tpu_custom_call" | custom-call | tf_op jit(solution)/shard_map/assemble/pallas_call | solution.py:70
  657.6 9.3 fusion.93
  671.8 7.0 convolution_convert_fusion
  678.8 11.9 convert_reduce_fusion
  690.7 7.9 convolution_convert_fusion.1
  698.7 5.8 multiply_reduce_fusion.1
  713.3 14.5 %fusion.1 = (f32[2,12,512]{2,1,0:T(8,128)S(1)}, f32[2,12,512,512]{2,3,1,0:T(8,128)}) fusion(bf16[2,12,512,512]{2,3,1,0:T(8,128)(2,1)} %copy-done.2, f32[2,512,12,3,64]{1,4,3,2,0:T(8,128)} %bitcast.347, f32[12,64]{1,0:T(8,128)S(1)} %get-tuple-element.152, bf16[2,512,12,64]{1,0,3,2:T(2,128)(2,1)S(1)} %reshape.317), kind=kOutput, calls=%fused_computation.3 | convolution fusion | flops 825741312 | bytes 42519552 | tf_op jit(solution)/shard_map/bqhd,bkhd->bhqk/dot_general | solution.py:205
  727.8 17.2 %fusion.2 = bf16[2,12,512,512]{2,3,1,0:T(8,128)(2,1)S(1)} fusion(f32[2,12,512,512]{2,3,1,0:T(8,128)} %get-tuple-element.175, f32[2,12,512]{2,1,0:T(8,128)S(1)} %get-tuple-element.174, f32[2,12,512,512]{2,3,1,0:T(8,128)} %get-tuple-element.164, f32[2,12,512]{2,1,0:T(8,128)S(1)} %get-tuple-element.163), kind=kLoop, calls=%fused_computation.4 | loop fusion | flops 37748736 | bytes 63012864 | tf_op jit(solution)/shard_map/convert_element_type | solution.py:206
  753.3 9.4 multiply_bitcast_fusion
  762.7 8.6 convolution_bitcast_fusion.1
  776.0 6.0 split_parts.6
  786.2 145.0 %split_parts.9 = (bf16[2,2,4,96,768]{4,3,2,1,0:T(8,128)(2,1)}, bf16[2,2,4,96,768]{4,3,2,1,0:T(8,128)(2,1)}) custom-call(s32[4]{0:T(128)} %pad_add_fusion.where_ref, bf16[32,96,768]{2,1,0:T(8,128)(2,1)} %bitcast.358), custom_call_target="tpu_custom_call" | custom-call | tf_op jit(solution)/shard_map/split_parts/pallas_call | solution.py:96
  931.5 37.8 %split_parts.7 = (bf16[2,2,4,24,768]{4,3,2,1,0:T(8,128)(2,1)}, bf16[2,2,4,24,768]{4,3,2,1,0:T(8,128)(2,1)}) custom-call(s32[4]{0:T(128)} %pad_add_fusion.where_ref, bf16[32,24,768]{2,1,0:T(8,128)(2,1)} %bitcast.374), custom_call_target="tpu_custom_call" | custom-call | tf_op jit(solution)/shard_map/split_parts/pallas_call | solution.py:96
  969.7 9.4 copy.73
  979.1 8.7 convert_element_type.380
  990.5 6.7 convert_bitcast_fusion
  1005.8 121.3 %split_parts.5 = (bf16[2,2,4,96,576]{4,3,2,1,0:T(8,128)(2,1)}, bf16[2,2,4,96,576]{4,3,2,1,0:T(8,128)(2,1)}) custom-call(s32[4]{0:T(128)} %pad_add_fusion.where_ref, bf16[32,96,576]{2,1,0:T(8,128)(2,1)} %bitcast.355), custom_call_target="tpu_custom_call" | custom-call | tf_op jit(solution)/shard_map/split_parts/pallas_call | solution.py:96
  1130.0 9.0 fusion.19
  1139.1 145.1 %split_parts.8 = (bf16[2,2,4,24,3072]{4,3,2,1,0:T(8,128)(2,1)}, bf16[2,2,4,24,3072]{4,3,2,1,0:T(8,128)(2,1)}) custom-call(s32[4]{0:T(128)} %pad_add_fusion.where_ref, bf16[32,24,3072]{2,1,0:T(8,128)(2,1)} %bitcast.357), custom_call_target="tpu_custom_call" | custom-call | tf_op jit(solution)/shard_map/split_parts/pallas_call | solution.py:96
  1328.8 5.9 collective-permute-done.62
  1351.0 8.8 collective-permute-done.94
  (476 shorter events, 258.9 us)
Async XLA Ops:
  27.5 30.9 %collective-permute-start.36 = (bf16[1,24,3072]{2,1,0:T(8,128)(2,1)}, bf16[1,24,3072]{2,1,0:T(8,128)(2,1)S(1)}, u32[]{:S(2)}, u32[]{:S(2)}) collective-permute-start(bf16[1,24,3072]{2,1,0:T(8,128)(2,1)} %bitcast.382), channel_id=1, source_target_pairs={{0,8},{1,9},{2,10},{3,11},{4,12},{5,13},{6,14},{7,15},{8,16},{9,17... | collective-permute-start | bytes 442376 | tf_op jit(solution)/shard_map/ppermute | solution.py:27
  28.1 30.9 %collective-permute-start.37 = (bf16[1,24,3072]{2,1,0:T(8,128)(2,1)}, bf16[1,24,3072]{2,1,0:T(8,128)(2,1)S(1)}, u32[]{:S(2)}, u32[]{:S(2)}) collective-permute-start(bf16[1,24,3072]{2,1,0:T(8,128)(2,1)} %bitcast.383), channel_id=1, source_target_pairs={{0,16},{1,17},{2,18},{3,19},{4,20},{5,21},{6,22},{7,23},{8,24},{9,... | collective-permute-start | bytes 442376 | tf_op jit(solution)/shard_map/ppermute | solution.py:27
  31.9 30.5 %collective-permute-start.27 = (bf16[4,24,768]{2,1,0:T(8,128)(2,1)S(1)}, bf16[4,24,768]{2,1,0:T(8,128)(2,1)S(1)}, u32[]{:S(2)}, u32[]{:S(2)}) collective-permute-start(bf16[4,24,768]{2,1,0:T(8,128)(2,1)S(1)} %pad_maximum_fusion.9.refs_0_), channel_id=1, source_target_pairs={{0,4},{1,5},{2,6},{3,7},{4,0},{5,1},{6,2},{7,3},{8,12},{9,13},{10,... | collective-permute-start | bytes 442376 | tf_op jit(solution)/shard_map/ppermute | solution.py:27
  81.8 31.0 %collective-permute-start.39 = (bf16[4,24,3072]{2,1,0:T(8,128)(2,1)S(1)}, bf16[4,24,3072]{2,1,0:T(8,128)(2,1)}, u32[]{:S(2)}, u32[]{:S(2)}) collective-permute-start(bf16[4,24,3072]{2,1,0:T(8,128)(2,1)S(1)} %pad_maximum_fusion.refs_0_), channel_id=1, source_target_pairs={{0,4},{1,5},{2,6},{3,7},{4,0},{5,1},{6,2},{7,3},{8,12},{9,13},{10,... | collective-permute-start | bytes 1769480 | tf_op jit(solution)/shard_map/ppermute | solution.py:27
  82.3 31.0 %collective-permute-start.40 = (bf16[4,24,3072]{2,1,0:T(8,128)(2,1)S(1)}, bf16[4,24,3072]{2,1,0:T(8,128)(2,1)}, u32[]{:S(2)}, u32[]{:S(2)}) collective-permute-start(bf16[4,24,3072]{2,1,0:T(8,128)(2,1)S(1)} %pad_maximum_fusion.refs_0_), channel_id=1, source_target_pairs={{0,2},{1,3},{2,0},{3,1},{4,6},{5,7},{6,4},{7,5},{8,10},{9,11},{10,... | collective-permute-start | bytes 1769480 | tf_op jit(solution)/shard_map/ppermute | solution.py:27
  83.8 30.0 %collective-permute-start.51 = (bf16[4,96,768]{2,1,0:T(8,128)(2,1)S(1)}, bf16[4,96,768]{2,1,0:T(8,128)(2,1)}, u32[]{:S(2)}, u32[]{:S(2)}) collective-permute-start(bf16[4,96,768]{2,1,0:T(8,128)(2,1)S(1)} %pad_maximum_fusion.1.refs_0_), channel_id=1, source_target_pairs={{0,4},{1,5},{2,6},{3,7},{4,0},{5,1},{6,2},{7,3},{8,12},{9,13},{10,... | collective-permute-start | bytes 1769480 | tf_op jit(solution)/shard_map/ppermute | solution.py:27
  86.1 34.7 %collective-permute-start.52 = (bf16[4,96,768]{2,1,0:T(8,128)(2,1)S(1)}, bf16[4,96,768]{2,1,0:T(8,128)(2,1)}, u32[]{:S(2)}, u32[]{:S(2)}) collective-permute-start(bf16[4,96,768]{2,1,0:T(8,128)(2,1)S(1)} %pad_maximum_fusion.1.refs_0_), channel_id=1, source_target_pairs={{0,2},{1,3},{2,0},{3,1},{4,6},{5,7},{6,4},{7,5},{8,10},{9,11},{10,... | collective-permute-start | bytes 1769480 | tf_op jit(solution)/shard_map/ppermute | solution.py:27
  112.2 58.5 %collective-permute-start.7 = (bf16[4,96,576]{2,1,0:T(8,128)(2,1)S(1)}, bf16[4,96,576]{2,1,0:T(8,128)(2,1)}, u32[]{:S(2)}, u32[]{:S(2)}) collective-permute-start(bf16[4,96,576]{2,1,0:T(8,128)(2,1)S(1)} %pad_maximum_fusion.6.refs_0_), channel_id=1, source_target_pairs={{0,1},{1,0},{2,3},{3,2},{4,5},{5,4},{6,7},{7,6},{8,9},{9,8},{10,11... | collective-permute-start | bytes 1327112 | tf_op jit(solution)/shard_map/ppermute | solution.py:27
  113.8 58.4 %collective-permute-start.8 = (bf16[4,96,576]{2,1,0:T(8,128)(2,1)}, bf16[4,96,576]{2,1,0:T(8,128)(2,1)}, u32[]{:S(2)}, u32[]{:S(2)}) collective-permute-start(bf16[4,96,576]{2,1,0:T(8,128)(2,1)} %copy-done.22), channel_id=1, source_target_pairs={{0,1},{1,0},{2,3},{3,2},{4,5},{5,4},{6,7},{7,6},{8,9},{9,8},{10,11... | collective-permute-start | bytes 1327112 | tf_op jit(solution)/shard_map/ppermute | solution.py:27
  120.8 52.9 %collective-permute-start.9 = (bf16[4,96,576]{2,1,0:T(8,128)(2,1)}, bf16[4,96,576]{2,1,0:T(8,128)(2,1)}, u32[]{:S(2)}, u32[]{:S(2)}) collective-permute-start(bf16[4,96,576]{2,1,0:T(8,128)(2,1)} %copy-done.23), channel_id=1, source_target_pairs={{0,1},{1,0},{2,3},{3,2},{4,5},{5,4},{6,7},{7,6},{8,9},{9,8},{10,11... | collective-permute-start | bytes 1327112 | tf_op jit(solution)/shard_map/ppermute | solution.py:27
  124.2 47.0 %collective-permute-start.10 = (bf16[2,96,576]{2,1,0:T(8,128)(2,1)S(1)}, bf16[2,96,576]{2,1,0:T(8,128)(2,1)}, u32[]{:S(2)}, u32[]{:S(2)}) collective-permute-start(bf16[2,96,576]{2,1,0:T(8,128)(2,1)S(1)} %collective-permute-done.5.refs_3_), channel_id=1, source_target_pairs={{0,1},{1,0},{2,3},{3,2},{4,5},{5,4},{6,7},{7,6},{8,9},{9,8},{10,11... | collective-permute-start | bytes 663560 | tf_op jit(solution)/shard_map/ppermute | solution.py:27
  124.7 47.0 %collective-permute-start.11 = (bf16[2,96,576]{2,1,0:T(8,128)(2,1)}, bf16[2,96,576]{2,1,0:T(8,128)(2,1)}, u32[]{:S(2)}, u32[]{:S(2)}) collective-permute-start(bf16[2,96,576]{2,1,0:T(8,128)(2,1)} %collective-permute-done.6.refs_4_), channel_id=1, source_target_pairs={{0,1},{1,0},{2,3},{3,2},{4,5},{5,4},{6,7},{7,6},{8,9},{9,8},{10,11... | collective-permute-start | bytes 663560 | tf_op jit(solution)/shard_map/ppermute | solution.py:27
  170.7 172.6 %collective-permute-start.43 = (bf16[4,24,3072]{2,1,0:T(8,128)(2,1)S(1)}, bf16[4,24,3072]{2,1,0:T(8,128)(2,1)}, u32[]{:S(2)}, u32[]{:S(2)}) collective-permute-start(bf16[4,24,3072]{2,1,0:T(8,128)(2,1)S(1)} %pad_maximum_fusion.refs_0_), channel_id=1, source_target_pairs={{0,1},{1,0},{2,3},{3,2},{4,5},{5,4},{6,7},{7,6},{8,9},{9,8},{10,11... | collective-permute-start | bytes 1769480 | tf_op jit(solution)/shard_map/ppermute | solution.py:27
  171.2 172.7 %collective-permute-start.41 = (bf16[2,24,3072]{2,1,0:T(8,128)(2,1)}, bf16[2,24,3072]{2,1,0:T(8,128)(2,1)S(1)}, u32[]{:S(2)}, u32[]{:S(2)}) collective-permute-start(bf16[2,24,3072]{2,1,0:T(8,128)(2,1)} %slice.513), channel_id=1, source_target_pairs={{0,2},{1,3},{2,0},{3,1},{4,6},{5,7},{6,4},{7,5},{8,10},{9,11},{10,... | collective-permute-start | bytes 884744 | tf_op jit(solution)/shard_map/ppermute | solution.py:27
  171.7 173.8 %collective-permute-start.42 = (bf16[2,24,3072]{2,1,0:T(8,128)(2,1)}, bf16[2,24,3072]{2,1,0:T(8,128)(2,1)}, u32[]{:S(2)}, u32[]{:S(2)}) collective-permute-start(bf16[2,24,3072]{2,1,0:T(8,128)(2,1)} %slice.514), channel_id=1, source_target_pairs={{0,4},{1,5},{2,6},{3,7},{4,0},{5,1},{6,2},{7,3},{8,12},{9,13},{10,... | collective-permute-start | bytes 884744 | tf_op jit(solution)/shard_map/ppermute | solution.py:27
  172.2 173.3 %collective-permute-start.53 = (bf16[2,96,768]{2,1,0:T(8,128)(2,1)}, bf16[2,96,768]{2,1,0:T(8,128)(2,1)S(1)}, u32[]{:S(2)}, u32[]{:S(2)}) collective-permute-start(bf16[2,96,768]{2,1,0:T(8,128)(2,1)} %slice.516), channel_id=1, source_target_pairs={{0,2},{1,3},{2,0},{3,1},{4,6},{5,7},{6,4},{7,5},{8,10},{9,11},{10,... | collective-permute-start | bytes 884744 | tf_op jit(solution)/shard_map/ppermute | solution.py:27
  173.7 179.3 %collective-permute-start.44 = (bf16[4,24,3072]{2,1,0:T(8,128)(2,1)}, bf16[4,24,3072]{2,1,0:T(8,128)(2,1)}, u32[]{:S(2)}, u32[]{:S(2)}) collective-permute-start(bf16[4,24,3072]{2,1,0:T(8,128)(2,1)} %collective-permute-done.39.refs_1_), channel_id=1, source_target_pairs={{0,1},{1,0},{2,3},{3,2},{4,5},{5,4},{6,7},{7,6},{8,9},{9,8},{10,11... | collective-permute-start | bytes 1769480 | tf_op jit(solution)/shard_map/ppermute | solution.py:27
  353.0 159.5 %collective-permute-start.55 = (bf16[4,96,768]{2,1,0:T(8,128)(2,1)S(1)}, bf16[4,96,768]{2,1,0:T(8,128)(2,1)}, u32[]{:S(2)}, u32[]{:S(2)}) collective-permute-start(bf16[4,96,768]{2,1,0:T(8,128)(2,1)S(1)} %pad_maximum_fusion.1.refs_0_), channel_id=1, source_target_pairs={{0,1},{1,0},{2,3},{3,2},{4,5},{5,4},{6,7},{7,6},{8,9},{9,8},{10,11... | collective-permute-start | bytes 1769480 | tf_op jit(solution)/shard_map/ppermute | solution.py:27
  353.0 159.5 %collective-permute-start.56 = (bf16[4,96,768]{2,1,0:T(8,128)(2,1)}, bf16[4,96,768]{2,1,0:T(8,128)(2,1)}, u32[]{:S(2)}, u32[]{:S(2)}) collective-permute-start(bf16[4,96,768]{2,1,0:T(8,128)(2,1)} %collective-permute-done.51.refs_1_), channel_id=1, source_target_pairs={{0,1},{1,0},{2,3},{3,2},{4,5},{5,4},{6,7},{7,6},{8,9},{9,8},{10,11... | collective-permute-start | bytes 1769480 | tf_op jit(solution)/shard_map/ppermute | solution.py:27
  353.5 159.0 %collective-permute-start.57 = (bf16[4,96,768]{2,1,0:T(8,128)(2,1)}, bf16[4,96,768]{2,1,0:T(8,128)(2,1)}, u32[]{:S(2)}, u32[]{:S(2)}) collective-permute-start(bf16[4,96,768]{2,1,0:T(8,128)(2,1)} %collective-permute-done.52.refs_2_), channel_id=1, source_target_pairs={{0,1},{1,0},{2,3},{3,2},{4,5},{5,4},{6,7},{7,6},{8,9},{9,8},{10,11... | collective-permute-start | bytes 1769480 | tf_op jit(solution)/shard_map/ppermute | solution.py:27
  354.4 158.1 %collective-permute-start.58 = (bf16[2,96,768]{2,1,0:T(8,128)(2,1)S(1)}, bf16[2,96,768]{2,1,0:T(8,128)(2,1)}, u32[]{:S(2)}, u32[]{:S(2)}) collective-permute-start(bf16[2,96,768]{2,1,0:T(8,128)(2,1)S(1)} %collective-permute-done.53.refs_3_), channel_id=1, source_target_pairs={{0,1},{1,0},{2,3},{3,2},{4,5},{5,4},{6,7},{7,6},{8,9},{9,8},{10,11... | collective-permute-start | bytes 884744 | tf_op jit(solution)/shard_map/ppermute | solution.py:27
  354.8 157.8 %collective-permute-start.59 = (bf16[2,96,768]{2,1,0:T(8,128)(2,1)}, bf16[2,96,768]{2,1,0:T(8,128)(2,1)}, u32[]{:S(2)}, u32[]{:S(2)}) collective-permute-start(bf16[2,96,768]{2,1,0:T(8,128)(2,1)} %collective-permute-done.54.refs_4_), channel_id=1, source_target_pairs={{0,1},{1,0},{2,3},{3,2},{4,5},{5,4},{6,7},{7,6},{8,9},{9,8},{10,11... | collective-permute-start | bytes 884744 | tf_op jit(solution)/shard_map/ppermute | solution.py:27
  782.0 205.8 %collective-permute-start.68 = (f32[2,2,4,8,128]{4,3,2,1,0:T(8,128)}, f32[2,2,4,8,128]{4,3,2,1,0:T(8,128)S(1)}, u32[]{:S(2)}, u32[]{:S(2)}) collective-permute-start(f32[2,2,4,8,128]{4,3,2,1,0:T(8,128)} %get-tuple-element.27), channel_id=1, source_target_pairs={{0,1},{1,0},{2,3},{3,2},{4,5},{5,4},{6,7},{7,6},{8,9},{9,8},{10,11... | collective-permute-start | bytes 196616 | tf_op jit(solution)/shard_map/ppermute | solution.py:27
  931.2 390.3 %collective-permute-start.92 = (bf16[2,2,4,96,768]{4,3,2,1,0:T(8,128)(2,1)}, bf16[2,2,4,96,768]{4,3,2,1,0:T(8,128)(2,1)}, u32[]{:S(2)}, u32[]{:S(2)}) collective-permute-start(bf16[2,2,4,96,768]{4,3,2,1,0:T(8,128)(2,1)} %get-tuple-element.33), channel_id=1, source_target_pairs={{0,1},{1,0},{2,3},{3,2},{4,5},{5,4},{6,7},{7,6},{8,9},{9,8},{10,11... | collective-permute-start | bytes 7077896 | tf_op jit(solution)/shard_map/ppermute | solution.py:27
  969.3 319.1 %collective-permute-start.76 = (bf16[2,2,4,24,768]{4,3,2,1,0:T(8,128)(2,1)}, bf16[2,2,4,24,768]{4,3,2,1,0:T(8,128)(2,1)}, u32[]{:S(2)}, u32[]{:S(2)}) collective-permute-start(bf16[2,2,4,24,768]{4,3,2,1,0:T(8,128)(2,1)} %get-tuple-element.29), channel_id=1, source_target_pairs={{0,1},{1,0},{2,3},{3,2},{4,5},{5,4},{6,7},{7,6},{8,9},{9,8},{10,11... | collective-permute-start | bytes 1769480 | tf_op jit(solution)/shard_map/ppermute | solution.py:27
  988.5 138.7 %collective-permute-start.69 = (f32[2,8,128]{2,1,0:T(8,128)}, f32[2,8,128]{2,1,0:T(8,128)}, u32[]{:S(2)}, u32[]{:S(2)}) collective-permute-start(f32[2,8,128]{2,1,0:T(8,128)} %get-tuple-element.137), channel_id=1, source_target_pairs={{0,2},{1,3},{2,0},{3,1},{4,6},{5,7},{6,4},{7,5},{8,10},{9,11},{10,... | collective-permute-start | bytes 24584 | tf_op jit(solution)/shard_map/ppermute | solution.py:27
  989.0 138.2 %collective-permute-start.71 = (f32[2,8,128]{2,1,0:T(8,128)}, f32[2,8,128]{2,1,0:T(8,128)}, u32[]{:S(2)}, u32[]{:S(2)}) collective-permute-start(f32[2,8,128]{2,1,0:T(8,128)} %get-tuple-element.138), channel_id=1, source_target_pairs={{0,4},{1,5},{2,6},{3,7},{4,0},{5,1},{6,2},{7,3},{8,12},{9,13},{10,... | collective-permute-start | bytes 24584 | tf_op jit(solution)/shard_map/ppermute | solution.py:27
  1127.1 179.7 %collective-permute-start.60 = (bf16[2,2,4,96,576]{4,3,2,1,0:T(8,128)(2,1)}, bf16[2,2,4,96,576]{4,3,2,1,0:T(8,128)(2,1)}, u32[]{:S(2)}, u32[]{:S(2)}) collective-permute-start(bf16[2,2,4,96,576]{4,3,2,1,0:T(8,128)(2,1)} %get-tuple-element.25), channel_id=1, source_target_pairs={{0,1},{1,0},{2,3},{3,2},{4,5},{5,4},{6,7},{7,6},{8,9},{9,8},{10,11... | collective-permute-start | bytes 5308424 | tf_op jit(solution)/shard_map/ppermute | solution.py:27
  1127.9 156.3 %collective-permute-start.70 = (f32[4,8,128]{2,1,0:T(8,128)S(1)}, f32[4,8,128]{2,1,0:T(8,128)S(1)}, u32[]{:S(2)}, u32[]{:S(2)}) collective-permute-start(f32[4,8,128]{2,1,0:T(8,128)S(1)} %pad_maximum_fusion.12), channel_id=1, source_target_pairs={{0,4},{1,5},{2,6},{3,7},{4,0},{5,1},{6,2},{7,3},{8,12},{9,13},{10,... | collective-permute-start | bytes 49160 | tf_op jit(solution)/shard_map/ppermute | solution.py:27
  1128.5 155.7 %collective-permute-start.72 = (f32[4,8,128]{2,1,0:T(8,128)S(1)}, f32[4,8,128]{2,1,0:T(8,128)S(1)}, u32[]{:S(2)}, u32[]{:S(2)}) collective-permute-start(f32[4,8,128]{2,1,0:T(8,128)S(1)} %pad_maximum_fusion.13), channel_id=1, source_target_pairs={{0,2},{1,3},{2,0},{3,1},{4,6},{5,7},{6,4},{7,5},{8,10},{9,11},{10,... | collective-permute-start | bytes 49160 | tf_op jit(solution)/shard_map/ppermute | solution.py:27
  1290.5 37.0 %collective-permute-start.84 = (bf16[2,2,4,24,3072]{4,3,2,1,0:T(8,128)(2,1)}, bf16[2,2,4,24,3072]{4,3,2,1,0:T(8,128)(2,1)S(1)}, u32[]{:S(2)}, u32[]{:S(2)}) collective-permute-start(bf16[2,2,4,24,3072]{4,3,2,1,0:T(8,128)(2,1)} %get-tuple-element.31), channel_id=1, source_target_pairs={{0,1},{1,0},{2,3},{3,2},{4,5},{5,4},{6,7},{7,6},{8,9},{9,8},{10,11... | collective-permute-start | bytes 7077896 | tf_op jit(solution)/shard_map/ppermute | solution.py:27
  1347.6 18.5 %collective-permute-start.86 = (bf16[4,24,3072]{2,1,0:T(8,128)(2,1)S(1)}, bf16[4,24,3072]{2,1,0:T(8,128)(2,1)S(1)}, u32[]{:S(2)}, u32[]{:S(2)}) collective-permute-start(bf16[4,24,3072]{2,1,0:T(8,128)(2,1)S(1)} %pad_maximum_fusion.2), channel_id=1, source_target_pairs={{0,4},{1,5},{2,6},{3,7},{4,0},{5,1},{6,2},{7,3},{8,12},{9,13},{10,... | collective-permute-start | bytes 1769480 | tf_op jit(solution)/shard_map/ppermute | solution.py:27
  (145 other events, 3251.8 us)

commit v2 on v1

--- a/solution.py
+++ b/solution.py
@@ -12,116 +12,101 @@
 F32 = jnp.float32
 
 
-def flat(z, y, x, c):
-    return ((z * 2 + y) * 2 + x) * 2 + c
-
-
-def move(value, dz=0, dy=0, dx=0, dc=0):
-    pairs = [
-        (flat(z, y, x, c), flat((z + dz) % 4, y ^ dy, x ^ dx, c ^ dc))
-        for z in range(4)
-        for y in range(2)
-        for x in range(2)
-        for c in range(2)
-    ]
-    return lax.ppermute(value, AXES, pairs)
-
-
-def coords():
-    dp, head = lax.axis_index("dp"), lax.axis_index("head")
-    return jnp.stack([dp // 2, dp % 2, head // 2, head % 2]).astype(jnp.int32)
-
-
-PIECES = [
-    (ry, rx, rc, first, count)
-    for rc in (0, 1)
-    for ry, rx, first, count in ((0, 0, 0, 4), (1, 0, 0, 4), (0, 1, 0, 4), (1, 1, 0, 2), (1, 1, 2, 2))
-]
-
-
-def gather_pieces(shard):
+Z_FAR, Z_NEAR, Y, X, CORE = 16, 8, 4, 2, 1
+
+
+def move(value, bit):
+    return lax.ppermute(value, AXES, [(d, d ^ bit) for d in range(32)])
+
+
+PLANE = [0, Z_NEAR, Z_FAR, Z_FAR | Z_NEAR]
+OFFSETS = PLANE + [Y | p for p in PLANE] + [X | p for p in PLANE] + [Y | X | p for p in PLANE]
+
+
+def gather_half(shard):
     own = shard[None]
-    plane = jnp.concatenate([own] + [move(own, dz=k) for k in (1, 2, 3)], axis=0)
-    from_y = move(plane, dy=1)
-    from_x = move(plane, dx=1)
-    far_a = move(from_y[:2], dx=1)
-    far_b = move(from_x[2:], dy=1)
-    mine = [plane, from_y, from_x, far_a, far_b]
-    return mine + [move(piece, dc=1) for piece in mine]
-
-
-def assemble(shard, where):
-    pieces = gather_pieces(shard)
-
-    def body(where_ref, *refs):
-        ins, out, sems = refs[: len(PIECES)], refs[len(PIECES)], refs[len(PIECES) + 1]
-        z, y, x, c = (where_ref[i] for i in range(4))
+    pair = jnp.concatenate([own, move(own, Z_NEAR)], axis=0)
+    plane = jnp.concatenate([pair, move(pair, Z_FAR)], axis=0)
+    from_y = move(plane, Y)
+    from_x = move(plane, X)
+    far_a = move(from_y[:2], X)
+    far_b = move(from_x[2:], Y)
+    return jnp.concatenate([plane, from_y, from_x, far_a, far_b], axis=0)
+
+
+def device_index():
+    return (lax.axis_index("dp") * lax.axis_size("head") + lax.axis_index("head")).astype(jnp.int32).reshape(1)
+
+
+def assemble(shard, me, outs, targets):
+    mine = gather_half(shard)
+    theirs = move(mine, CORE)
+
+    def body(me_ref, mine_ref, theirs_ref, *rest):
+        out_refs, sems = rest[:-1], rest[-1]
         copies = []
-        for ref, (ry, rx, rc, first, count) in zip(ins, PIECES):
-            for k in range(count):
-                source_z = lax.rem(z + 4 - (first + k), 4)
-                target = flat(source_z, y ^ ry, x ^ rx, c ^ rc)
-                copy = pltpu.make_async_copy(ref.at[k], out.at[target], sems.at[len(copies)])
-                copy.start()
-                copies.append(copy)
+        for core, ref in ((0, mine_ref), (CORE, theirs_ref)):
+            for k, offset in enumerate(OFFSETS):
+                for source, target in targets(ref.at[k], out_refs, me_ref[0] ^ (offset | core)):
+                    copy = pltpu.make_async_copy(source, target, sems.at[len(copies)])
+                    copy.start()
+                    copies.append(copy)
         for copy in copies:
             copy.wait()
 
+    hbm = pl.BlockSpec(memory_space=pl.ANY)
     return pl.pallas_call(
         body,
-        out_shape=jax.ShapeDtypeStruct((32,) + shard.shape, shard.dtype),
-        in_specs=[pl.BlockSpec(memory_space=pltpu.SMEM)] + [pl.BlockSpec(memory_space=pl.ANY)] * len(pieces),
-        out_specs=pl.BlockSpec(memory_space=pl.ANY),
-        scratch_shapes=[pltpu.SemaphoreType.DMA((32,))],
+        out_shape=outs,
+        in_specs=[pl.BlockSpec(memory_space=pltpu.SMEM), hbm, hbm],
+        out_specs=[pl.BlockSpec(memory_space=pltpu.VMEM)] * len(outs),
+        scratch_shapes=[pltpu.SemaphoreType.DMA((32 * len(outs),))],
         name="assemble",
-    )(where, *pieces)
-
-
-def split_parts(full, where):
-    def body(where_ref, full_ref, keep_ref, send_ref, sems):
-        z, y, x, c = (where_ref[i] for i in range(4))
+    )(me, mine, theirs)
+
+
+def split_parts(fulls, me, block, sources):
+    def body(me_ref, *rest):
+        full_refs, (keep_ref, send_ref, sems) = rest[: len(fulls)], rest[len(fulls) :]
         copies = []
-        for rc, out in ((0, keep_ref), (1, send_ref)):
-            for ry in (0, 1):
-                for rx in (0, 1):
-                    for rz in range(4):
-                        source = flat(lax.rem(z + rz, 4), y ^ ry, x ^ rx, c ^ rc)
-                        copy = pltpu.make_async_copy(full_ref.at[source], out.at[ry, rx, rz], sems.at[len(copies)])
-                        copy.start()
-                        copies.append(copy)
+        for core, out in ((0, keep_ref), (CORE, send_ref)):
+            for k, offset in enumerate(OFFSETS):
+                for source, target in sources(full_refs, out.at[k], me_ref[0] ^ (offset | core)):
+                    copy = pltpu.make_async_copy(source, target, sems.at[len(copies)])
+                    copy.start()
+                    copies.append(copy)
         for copy in copies:
             copy.wait()
 
-    half = jax.ShapeDtypeStruct((2, 2, 4) + full.shape[1:], full.dtype)
+    half = jax.ShapeDtypeStruct((16,) + block, LOW)
+    hbm = pl.BlockSpec(memory_space=pl.ANY)
     return pl.pallas_call(
         body,
         out_shape=(half, half),
-        in_specs=[pl.BlockSpec(memory_space=pltpu.SMEM), pl.BlockSpec(memory_space=pl.ANY)],
-        out_specs=(pl.BlockSpec(memory_space=pl.ANY), pl.BlockSpec(memory_space=pl.ANY)),
-        scratch_shapes=[pltpu.SemaphoreType.DMA((32,))],
+        in_specs=[pl.BlockSpec(memory_space=pltpu.SMEM)] + [pl.BlockSpec(memory_space=pltpu.VMEM)] * len(fulls),
+        out_specs=(hbm, hbm),
+        scratch_shapes=[pltpu.SemaphoreType.DMA((32 * len(fulls),))],
         name="split_parts",
-    )(where, full)
+    )(me, *fulls)
+
+
+def add(first, *rest):
+    total = first.astype(F32)
+    for term in rest:
+        total = total + term.astype(F32)
+    return total
 
 
 def reduce_parts(kept, sent):
-    kind = kept.dtype
-
-    def add(first, *rest):
-        total = first.astype(F32)
-        for term in rest:
-            total = total + term.astype(F32)
-        return total
-
-    here = add(kept, move(sent, dc=1)).astype(kind)
-    far = here[1, 1]
-    near_y, near_x = here[1, 0], here[0, 1]
-    via_x = move(far[:2], dx=1)
-    via_y = move(far[2:], dy=1)
-    to_y = jnp.concatenate([add(near_y[:2], via_x).astype(kind), near_y[2:]], axis=0)
-    to_x = jnp.concatenate([near_x[:2], add(near_x[2:], via_y).astype(kind)], axis=0)
-    plane = add(here[0, 0], move(to_y, dy=1), move(to_x, dx=1))
-    low = plane.astype(kind)
-    return add(plane[0], *[move(low[k], dz=k) for k in (1, 2, 3)])
+    here = add(kept, move(sent, CORE)).astype(LOW)
+    plane, near_y, near_x, far = here[:4], here[4:8], here[8:12], here[12:]
+    via_x = move(far[:2], X)
+    via_y = move(far[2:], Y)
+    to_y = jnp.concatenate([add(near_y[:2], via_x).astype(LOW), near_y[2:]], axis=0)
+    to_x = jnp.concatenate([near_x[:2], add(near_x[2:], via_y).astype(LOW)], axis=0)
+    plane = add(plane, move(to_y, Y), move(to_x, X))
+    pair = add(plane[:2], move(plane[2:].astype(LOW), Z_FAR))
+    return add(pair[0], move(pair[1].astype(LOW), Z_NEAR))
 
 
 def norm_stats(hidden):
@@ -228,34 +213,62 @@
     inner_weight, inner_shift, outer_weight, outer_shift, second_gain, second_shift = params[6:]
     micro, local, slots, features = tokens.shape
     dp, groups = lax.axis_size("dp"), lax.axis_size("head")
+    devices = dp * groups
     staged = (dp, groups) == (8, 4)
     position = lax.axis_index("head")
-    where = coords()
+    me = device_index()
     own = lax.dynamic_slice_in_dim(lengths, position * local, local, 1).reshape(micro * local)
     rows = tokens.reshape(micro * local, slots, features)
     upstream = cotangent.reshape(micro * local, slots, features)
+    depth, width = qkv_weight.shape
+    hidden = inner_weight.shape[1]
+    share = inner_weight.shape[0]
 
     vectors = [proj_shift, first_gain, first_shift, outer_shift, second_gain, second_shift, inner_shift, qv_shift.reshape(-1)]
     lens = [v.shape[0] for v in vectors]
     total = sum(lens)
-    padded = -(-total // 1024) * 1024
-    small = jnp.pad(jnp.concatenate(vectors), (0, padded - total)).reshape(8, padded // 8)
-
-    def everyone(shard):
-        if staged:
-            return assemble(shard, where)
-        return lax.all_gather(shard, AXES, axis=0)
-
-    qkv_all = everyone(qkv_weight)
-    small_all = everyone(small).reshape(dp * groups, padded)
-    proj = everyone(proj_weight).reshape(-1, features)
-    inner = everyone(inner_weight).reshape(features, -1)
-    outer = everyone(outer_weight).reshape(-1, features)
-    depth, width = qkv_weight.shape
-    qkv = qkv_all.reshape(dp, groups, depth, width).swapaxes(0, 1).reshape(groups, dp * depth, width)
+    small = jnp.pad(jnp.concatenate(vectors).reshape(1, total), ((0, 7), (0, width - total)))
+
+    if staged:
+        def qkv_targets(source, refs, device):
+            qkv_ref, small_ref = refs
+            return [
+                (source.at[pl.ds(0, depth)], qkv_ref.at[device % groups, device // groups]),
+                (source.at[pl.ds(depth, 8)], small_ref.at[device]),
+            ]
+
+        qkv, small_all = assemble(
+            jnp.concatenate([qkv_weight, small], axis=0), me,
+            [jax.ShapeDtypeStruct((groups, dp, depth, width), LOW), jax.ShapeDtypeStruct((devices, 8, width), LOW)],
+            qkv_targets,
+        )
+        qkv = qkv.reshape(groups, dp * depth, width)
+
+        def inner_targets(source, refs, device):
+            return [
+                (source.at[:, pl.ds(0, hidden)], refs[0].at[device]),
+                (source.at[:, pl.ds(hidden, features)], refs[1].at[device]),
+            ]
+
+        inner, proj = assemble(
+            jnp.concatenate([inner_weight, proj_weight], axis=1), me,
+            [jax.ShapeDtypeStruct((devices, share, hidden), LOW), jax.ShapeDtypeStruct((devices, share, features), LOW)],
+            inner_targets,
+        )
+        (outer,) = assemble(
+            outer_weight, me, [jax.ShapeDtypeStruct((devices,) + outer_weight.shape, LOW)],
+            lambda source, refs, device: [(source, refs[0].at[device])],
+        )
+    else:
+        def everyone(shard):
+            return lax.all_gather(shard, AXES, axis=0)
+
+        qkv = everyone(qkv_weight).reshape(dp, groups, depth, width).swapaxes(0, 1).reshape(groups, dp * depth, width)
+        small_all, inner, proj, outer = everyone(small), everyone(inner_weight), everyone(proj_weight), everyone(outer_weight)
+    inner, proj, outer = inner.reshape(features, hidden), proj.reshape(features, features), outer.reshape(hidden, features)
     pieces, at = [], 0
     for size in lens:
-        pieces.append(small_all[:, at : at + size].astype(F32))
+        pieces.append(small_all[:, 0, at : at + size].astype(F32))
         at += size
     full = [p.reshape(-1) for p in pieces[:-1]]
     shift = pieces[-1].reshape((dp, groups) + qv_shift.shape).transpose(1, 2, 0, 3).reshape(-1, 2 * DH)
@@ -265,24 +278,40 @@
         qkv_grad, qv_shift_grad, proj_grad, proj_shift_grad, gain_one_grad, shift_one_grad,
         inner_grad, inner_shift_grad, outer_grad, outer_shift_grad, gain_two_grad, shift_two_grad,
     ) = grads
-
-    def owner(grad):
-        if staged:
-            return reduce_parts(*split_parts(grad, where))
-        parts = lax.all_to_all(grad, AXES, 0, 0, tiled=True)
-        return jnp.sum(parts.astype(F32), axis=0)
-
-    devices = dp * groups
-    outer_out = owner(outer_grad.reshape((devices,) + outer_weight.shape))
-    inner_out = owner(inner_grad.reshape((devices,) + inner_weight.shape))
-    proj_out = owner(proj_grad.reshape((devices,) + proj_weight.shape))
-    qkv_blocks = qkv_grad.reshape(groups, dp, depth, width).swapaxes(0, 1)
-    qkv_out = owner(qkv_blocks.reshape(devices, depth, width))
     shift_blocks = qv_shift_grad.reshape(groups, qv_shift.shape[0], dp, qv_shift.shape[1]).transpose(2, 0, 1, 3)
     vector_grads = [proj_shift_grad, gain_one_grad, shift_one_grad, outer_shift_grad, gain_two_grad, shift_two_grad, inner_shift_grad, shift_blocks]
     small_grad = jnp.concatenate([g.reshape(devices, -1) for g in vector_grads], axis=1)
-    small_grad = jnp.pad(small_grad, ((0, 0), (0, padded - total))).reshape(devices, 8, padded // 8)
-    small_out = owner(small_grad).reshape(padded)
+    small_grad = jnp.pad(small_grad.reshape(devices, 1, total), ((0, 0), (0, 7), (0, width - total)))
+    outer_grad = outer_grad.reshape((devices,) + outer_weight.shape)
+    inner_grad = inner_grad.reshape(devices, share, hidden)
+    proj_grad = proj_grad.reshape(devices, share, features)
+    qkv_grad = qkv_grad.reshape(groups, dp, depth, width)
+
+    if staged:
+        outer_out = reduce_parts(*split_parts(
+            [outer_grad], me, outer_weight.shape, lambda refs, target, device: [(refs[0].at[device], target)]))
+        inner_proj = reduce_parts(*split_parts(
+            [inner_grad, proj_grad], me, (share, hidden + features),
+            lambda refs, target, device: [
+                (refs[0].at[device], target.at[:, pl.ds(0, hidden)]),
+                (refs[1].at[device], target.at[:, pl.ds(hidden, features)]),
+            ]))
+        inner_out, proj_out = inner_proj[:, :hidden], inner_proj[:, hidden:]
+        qkv_small = reduce_parts(*split_parts(
+            [qkv_grad, small_grad.astype(LOW)], me, (depth + 8, width),
+            lambda refs, target, device: [
+                (refs[0].at[device % groups, device // groups], target.at[pl.ds(0, depth)]),
+                (refs[1].at[device], target.at[pl.ds(depth, 8)]),
+            ]))
+        qkv_out, small_out = qkv_small[:depth], qkv_small[depth]
+    else:
+        def owner(grad):
+            parts = lax.all_to_all(grad, AXES, 0, 0, tiled=True)
+            return jnp.sum(parts.astype(F32), axis=0)
+
+        outer_out, inner_out, proj_out = owner(outer_grad), owner(inner_grad), owner(proj_grad)
+        qkv_out = owner(qkv_grad.swapaxes(0, 1).reshape(devices, depth, width))
+        small_out = owner(small_grad)[0]
     outs, at = [], 0
     for size in lens:
         outs.append(small_out[at : at + size])

time: 1390 us -> 475 us (0.34)
  Pallas kernels: 908 us -> 31.3 us
  starting transfers between devices: 92.6 us -> 43.8 us
  waiting for transfers between devices: 90.5 us -> 119 us
  local copies, waits for them, and re-layouts: 90.6 us -> 72 us
    pallas_call x5 -> x3, Pallas kernels: 455 us -> 15.6 us  [split_parts(): pl.pallas_call(body, out_shape=(half, half), in_specs=[pl.BlockSpec(memor...]
    pallas_call x5 -> x3, Pallas kernels: 453 us -> 15.7 us  [assemble(): pl.pallas_call(body, out_shape=outs, in_specs=[pl.BlockSpec(memory_space=...]
    ppermute x100 -> x42, starting transfers between devices: 92.6 us -> 43.8 us  [move(): return lax.ppermute(value, AXES, [(d, d ^ bit) for d in range(32)])]
    ppermute x100 -> x42, waiting for transfers between devices: 90.5 us -> 119 us  [move(): return lax.ppermute(value, AXES, [(d, d ^ bit) for d in range(32)])]
  transfers between devices with their start and end apart: 100 -> 42, of which waited for: 28 -> 21; matrix products, arithmetic and copies ran while one was open for 11% -> 25% of each run, Pallas kernels for 55% -> 4%
where the time goes in v2:
time: 475 us; the launch traced here: 467 us
  matrix products  139 us (29%)
  waiting for transfers between devices  119 us (25%)
  local copies, waits for them, and re-layouts  72 us (15%)
  other arithmetic  60.4 us (13%)
  starting transfers between devices  43.8 us (9%)
  Pallas kernels  31.3 us (7%)
    ppermute x42, waiting for transfers between devices, move(): return lax.ppermute(value, AXES, [(d, d ^ bit) for d in range(32)])  119 us
    dot_general x9, matrix products, mm(): return lax.dot_general(a, b, (dims, ((), ())), preferred_element_type=F32)  61.3 us
    ppermute x42, starting transfers between devices, move(): return lax.ppermute(value, AXES, [(d, d ^ bit) for d in range(32)])  43.8 us
    unnamed x95, local copies, waits for them, and re-layouts  19.9 us
    convert_element_type x2, local copies, waits for them, and re-layouts, layer(): jnp.stack([query_grad, key_grad, value_grad], axis=3).astype(LOW)  18.1 us
    sub x1, matrix products, layer(): raised = jnp.exp(scores - highest)  17.5 us
    convert_element_type x1, other arithmetic, layer(): (soft * (soft_grad - jnp.sum(soft * soft_grad, axis=-1, keepdims=True)))....  16.9 us
    pallas_call x3, Pallas kernels, assemble(): pl.pallas_call(body, out_shape=outs, in_specs=[pl.BlockSpec(memory_space=...  15.7 us
  transfers between devices with their start and end apart: 42, of which 21 were waited for; matrix products, arithmetic and copies ran while one was open for 25% of the time, Pallas kernels for 4%

profile of v2, /device:TPU:0, one launch (start us, length us, event | category | flops | bytes accessed | tf_op | source)
XLA Modules:
  0.0 467.4 jit_solution(2943528244406549476)
XLA Ops:
  28.7 19.2 %collective-permute-done.1 = bf16[2,104,576]{2,1,0:T(8,128)(2,1)S(1)} collective-permute-done((bf16[2,104,576]{2,1,0:T(8,128)(2,1)S(1)}, bf16[2,104,576]{2,1,0:T(8,128)(2,1)S(1)}, u32[]{:S(2)}, u32[]{:S(2)}) %collective-permute-start.1) | collective-permute-done | bytes 239648 | tf_op jit(solution)/shard_map/ppermute | solution.py:19
  66.3 9.4 %collective-permute-done.16 = bf16[4,96,768]{2,1,0:T(8,128)(2,1)S(1)} collective-permute-done((bf16[4,96,768]{2,1,0:T(8,128)(2,1)S(1)}, bf16[4,96,768]{2,1,0:T(8,128)(2,1)S(1)}, u32[]{:S(2)}, u32[]{:S(2)}) %collective-permute-start.16) | collective-permute-done | bytes 589856 | tf_op jit(solution)/shard_map/ppermute | solution.py:19
  80.6 16.2 %collective-permute-done.4 = bf16[2,104,576]{2,1,0:T(8,128)(2,1)S(1)} collective-permute-done((bf16[2,104,576]{2,1,0:T(8,128)(2,1)S(1)}, bf16[2,104,576]{2,1,0:T(8,128)(2,1)S(1)}, u32[]{:S(2)}, u32[]{:S(2)}) %collective-permute-start.4) | collective-permute-done | bytes 239648 | tf_op jit(solution)/shard_map/ppermute | solution.py:19
  113.6 5.0 %assemble.3 = (bf16[4,8,96,576]{3,2,1,0:T(8,128)(2,1)}, bf16[32,8,576]{2,1,0:T(8,128)(2,1)}) custom-call(s32[1]{0:T(128)} %bitcast.1.me_ref, bf16[16,104,576]{2,1,0:T(8,128)(2,1)} %copy-done.16, bf16[16,104,576]{2,1,0:T(8,128)(2,1)} %copy-done.18), custom_call_target="tpu_custom_call" | custom-call | tf_op jit(solution)/shard_map/assemble/pallas_call | solution.py:58
  118.5 7.2 %convolution_bitcast_fusion = f32[2,512,4,576]{1,3,0,2:T(8,128)S(1)} fusion(bf16[4,768,576,1]{2,1,3,0:T(8,128)(2,1)} %bitcast.212, bf16[2,1,512,768]{3,2,1,0:T(8,128)(2,1)} %param.15), kind=kOutput, calls=%fused_computation.29 | convolution fusion | flops 3623878656 | bytes 14548992 | tf_op jit(solution)/shard_map/bsd,gde->bsge/dot_general | solution.py:145
  131.8 17.5 %fusion.60 = (f32[2,12,512]{2,1,0:T(8,128)S(1)}, f32[2,12,512,512]{2,3,1,0:T(8,128)}) fusion(pred[2,512]{1,0:T(4,128)(4,1)S(1)} %get-tuple-element.113, f32[2,512,12,3,64]{1,4,3,2,0:T(8,128)} %bitcast.178, f32[12,64]{1,0:T(8,128)S(1)} %get-tuple-element.110), kind=kOutput, calls=%fused_computation.183 | convolution fusion | flops 832045568 | bytes 29937664 | tf_op jit(solution)/shard_map/sub | solution.py:157
  149.3 10.6 %divide_convert_fusion = bf16[2,12,512,512]{2,3,1,0:T(8,128)(2,1)S(1)} fusion(f32[2,12,512,512]{2,3,1,0:T(8,128)} %get-tuple-element.115, f32[2,12,512]{2,1,0:T(8,128)S(1)} %get-tuple-element.114), kind=kLoop, calls=%fused_computation.5 | loop fusion | flops 12582912 | bytes 37797888 | tf_op jit(solution)/shard_map/convert_element_type | solution.py:158
  170.8 4.9 %assemble.5 = bf16[32,96,768]{2,1,0:T(8,128)(2,1)} custom-call(s32[1]{0:T(128)} %bitcast.1.me_ref, bf16[16,96,768]{2,1,0:T(8,128)(2,1)} %constant_dynamic-update-slice_fusion.14.mine_ref, bf16[16,96,768]{2,1,0:T(8,128)(2,1)} %collective-permute-done.20.theirs_ref), custom_call_target="tpu_custom_call" | custom-call | tf_op jit(solution)/shard_map/assemble/pallas_call | solution.py:58
  175.7 5.9 %assemble.4 = (bf16[32,24,3072]{2,1,0:T(8,128)(2,1)}, bf16[32,24,768]{2,1,0:T(8,128)(2,1)}) custom-call(s32[1]{0:T(128)} %bitcast.1.me_ref, bf16[16,24,3840]{2,1,0:T(8,128)(2,1)} %constant_dynamic-update-slice_fusion.7.mine_ref, bf16[16,24,3840]{2,1,0:T(8,128)(2,1)} %collective-permute-done.13.theirs_ref), custom_call_target="tpu_custom_call" | custom-call | tf_op jit(solution)/shard_map/assemble/pallas_call | solution.py:58
  185.7 9.5 %multiply_convert_fusion = (bf16[1024,3072]{1,0:T(8,128)(2,1)S(1)}, f32[1024,3072]{1,0:T(8,128)}) fusion(f32[3072]{0:T(1024)S(1)} %reshape.341, bf16[768,3072]{1,0:T(8,128)(2,1)S(1)} %bitcast.210, f32[1024,768]{1,0:T(8,128)S(1)} %get-tuple-element.117, f32[768]{0:T(1024)S(1)} %reshape.340, f32[768]{0:T(1024)S(1)} %reshape.339, ...), kind=kOutput, calls=%fused_computation.16 | convolution fusion | flops 4854644736 | bytes 26765312 | tf_op jit(solution)/shard_map/dot_general | solution.py:134
  195.3 5.4 %fusion.66 = (f32[1024]{0:T(1024)S(1)}, f32[1024,768]{1,0:T(8,128)S(1)}) fusion(f32[768]{0:T(1024)S(1)} %reshape.342, bf16[1024,3072]{1,0:T(8,128)(2,1)S(1)} %get-tuple-element.118, bf16[3072,768]{1,0:T(8,128)(2,1)S(1)} %bitcast.191, f32[768]{0:T(1024)S(1)} %reshape.340, f32[768]{0:T(1024)S(1)} %reshape.339, f32[1024]{0:T(1024)S(1)} %add_rsqrt_fusion.1, ...), kind=kOutput, calls=%fused_computation.185 | convolution fusion | flops 4837342208 | bytes 17323008 | tf_op jit(solution)/shard_map/dot_general | solution.py:134
  205.2 12.9 %fusion.67 = (bf16[3072]{0:T(1024)(128)(2,1)S(1)}, bf16[1024,3072]{1,0:T(8,128)(2,1)S(1)}) fusion(f32[1024,3072]{1,0:T(8,128)} %get-tuple-element.119, f32[3072]{0:T(1024)S(1)} %reshape.341, bf16[3072,768]{1,0:T(8,128)(2,1)S(1)} %bitcast.192, f32[1024,768]{1,0:T(8,128)S(1)} %get-tuple-element.79), kind=kOutput, calls=%fused_computation.186 | convolution fusion | flops 4870370304 | bytes 26757120 | tf_op jit(solution)/shard_map/dot_general | solution.py:134
  218.1 5.8 %multiply_reduce_fusion.1 = (bf16[768]{0:T(1024)(128)(2,1)S(1)}, f32[1024]{0:T(1024)S(1)}, f32[1024]{0:T(1024)S(1)}, bf16[768]{0:T(1024)(128)(2,1)S(1)}, f32[1024,768]{1,0:T(8,128)S(1)}) fusion(f32[1024,768]{1,0:T(8,128)S(1)} %get-tuple-element.117, f32[1024]{0:T(1024)S(1)} %add_rsqrt_fusion.1, f32[1024]{0:T(1024)S(1)} %broadcast_multiply_fusion.4, ...), kind=kOutput, calls=%fused_computation.41 | convolution fusion | flops 4839698432 | bytes 20469760 | tf_op jit(solution)/shard_map/dot_general | solution.py:134
  232.9 14.5 %fusion.1 = (f32[2,12,512]{2,1,0:T(8,128)S(1)}, f32[2,12,512,512]{2,3,1,0:T(8,128)}) fusion(bf16[2,12,512,512]{2,3,1,0:T(8,128)(2,1)} %copy-done.2, f32[2,512,12,3,64]{1,4,3,2,0:T(8,128)} %bitcast.179, f32[12,64]{1,0:T(8,128)S(1)} %get-tuple-element.109, bf16[2,512,12,64]{1,0,3,2:T(2,128)(2,1)S(1)} %reshape.320), kind=kOutput, calls=%fused_computation.3 | convolution fusion | flops 825741312 | bytes 42519552 | tf_op jit(solution)/shard_map/bqhd,bkhd->bhqk/dot_general | solution.py:190
  247.4 16.9 %fusion.2 = bf16[2,12,512,512]{2,3,1,0:T(8,128)(2,1)S(1)} fusion(f32[2,12,512,512]{2,3,1,0:T(8,128)} %get-tuple-element.124, f32[2,12,512]{2,1,0:T(8,128)S(1)} %get-tuple-element.123, f32[2,12,512,512]{2,3,1,0:T(8,128)} %get-tuple-element.115, f32[2,12,512]{2,1,0:T(8,128)S(1)} %get-tuple-element.114), kind=kLoop, calls=%fused_computation.4 | loop fusion | flops 37748736 | bytes 63012864 | tf_op jit(solution)/shard_map/convert_element_type | solution.py:191
  272.5 9.4 %multiply_bitcast_fusion = bf16[2,512,12,1,64]{1,4,2,0,3:T(8,128)(2,1)S(1)} fusion(bf16[2,12,512,512]{2,3,1,0:T(8,128)(2,1)} %copy-done.3, f32[2,512,12,3,64]{1,4,3,2,0:T(8,128)} %bitcast.180, f32[12,64]{1,0:T(8,128)S(1)} %get-tuple-element.110), kind=kOutput, calls=%fused_computation.42 | convolution fusion | flops 808452096 | bytes 17304576 | tf_op jit(solution)/shard_map/bhqk,bqhd->bkhd/dot_general | solution.py:193
  282.0 8.6 %convolution_bitcast_fusion.1 = bf16[2,512,12,1,64]{1,4,2,0,3:T(8,128)(2,1)S(1)} fusion(bf16[2,12,512,512]{2,3,1,0:T(8,128)(2,1)} %copy-done.2, bf16[2,512,12,64]{1,0,3,2:T(2,128)(2,1)S(1)} %reshape.320), kind=kOutput, calls=%fused_computation.62 | convolution fusion | flops 805306368 | bytes 15728640 | tf_op jit(solution)/shard_map/bhqk,bqhd->bkhd/dot_general | solution.py:194
  295.0 9.4 %copy.53 = bf16[2,512,12,3,64]{1,0,4,3,2:T(2,128)(2,1)} copy(bf16[2,512,12,3,64]{1,4,2,0,3:T(8,128)(2,1)} %get-tuple-element.77) | data formatting | bytes 9437184 | tf_op jit(solution)/shard_map/convert_element_type | solution.py:195
  304.4 8.7 %convert_element_type.376 = bf16[1024,4,576]{0,2,1:T(8,128)(2,1)} reshape(bf16[2,512,12,3,64]{1,0,4,3,2:T(2,128)(2,1)} %copy.53) | data formatting | bytes 9437184 | tf_op jit(solution)/shard_map/convert_element_type | solution.py:195
  313.1 6.7 %convert_bitcast_fusion = bf16[4,768,576]{1,2,0:T(8,128)(2,1)S(1)} fusion(bf16[1024,4,576]{0,2,1:T(8,128)(2,1)} %convert_element_type.376, bf16[1024,768,1]{1,0,2:T(8,128)(2,1)} %bitcast.215), kind=kOutput, calls=%fused_computation.27 | convolution fusion | flops 3625648128 | bytes 9830400 | tf_op jit(solution)/shard_map/nd,nge->gde/dot_general | solution.py:199
  330.8 10.3 %convolution_convert_fusion = bf16[3072,768]{1,0:T(8,128)(2,1)} fusion(bf16[1024,3072]{1,0:T(8,128)(2,1)} %copy-done.28, f32[1024,768]{1,0:T(8,128)S(1)} %copy-done.11), kind=kOutput, calls=%fused_computation.23 | convolution fusion | flops 4834983936 | bytes 14155776 | tf_op jit(solution)/shard_map/dot_general | solution.py:134
  341.1 4.9 %split_parts.5 = (bf16[16,96,768]{2,1,0:T(8,128)(2,1)}, bf16[16,96,768]{2,1,0:T(8,128)(2,1)}) custom-call(s32[1]{0:T(128)} %bitcast.1.me_ref, bf16[32,96,768]{2,1,0:T(8,128)(2,1)} %bitcast.194), custom_call_target="tpu_custom_call" | custom-call | tf_op jit(solution)/shard_map/split_parts/pallas_call | solution.py:83
  346.2 10.1 %convolution_convert_fusion.1 = bf16[768,3072]{1,0:T(8,128)(2,1)} fusion(bf16[1024,3072]{1,0:T(8,128)(2,1)} %copy-done.27, f32[1024,768]{1,0:T(8,128)S(1)} %copy-done.7, f32[768]{0:T(1024)S(1)} %copy-done.25, f32[768]{0:T(1024)S(1)} %reshape.339, f32[1024]{0:T(1024)S(1)} %add_rsqrt_fusion.1, f32[1024]{0:T(1024)S(1)} %broadcast_multiply_fusion.4), kind=kOutput, calls=%fused_computation.24 | convolution fusion | flops 4838129664 | bytes 14170112 | tf_op jit(solution)/shard_map/dot_general | solution.py:134
  363.8 5.8 %split_parts.4 = (bf16[16,24,3840]{2,1,0:T(8,128)(2,1)}, bf16[16,24,3840]{2,1,0:T(8,128)(2,1)}) custom-call(s32[1]{0:T(128)} %bitcast.1.me_ref, bf16[32,24,3072]{2,1,0:T(8,128)(2,1)} %bitcast.193, bf16[32,24,768]{2,1,0:T(8,128)(2,1)} %bitcast.201), custom_call_target="tpu_custom_call" | custom-call | tf_op jit(solution)/shard_map/split_parts/pallas_call | solution.py:83
  377.0 7.8 %fusion.19 = bf16[1024,768]{1,0:T(8,128)(2,1)} fusion(f32[1024,768]{1,0:T(8,128)S(1)} %copy-done.14, bf16[1024,4,576]{0,2,1:T(8,128)(2,1)S(1)} %bitcast.188, bf16[4,768,576]{2,1,0:T(8,128)(2,1)} %bitcast.213), kind=kOutput, calls=%fused_computation.38 | convolution fusion | flops 3625451520 | bytes 12976128 | tf_op jit(solution)/shard_map/nge,gde->nd/dot_general | solution.py:200
  386.9 5.3 %collective-permute-done.36 = bf16[2,96,768]{2,1,0:T(8,128)(2,1)S(1)} collective-permute-done((bf16[2,96,768]{2,1,0:T(8,128)(2,1)S(1)}, bf16[2,96,768]{2,1,0:T(8,128)(2,1)S(1)}, u32[]{:S(2)}, u32[]{:S(2)}) %collective-permute-start.36) | collective-permute-done | bytes 294944 | tf_op jit(solution)/shard_map/ppermute | solution.py:19
  393.8 6.7 %collective-permute-done.26 = bf16[2,104,576]{2,1,0:T(8,128)(2,1)S(1)} collective-permute-done((bf16[2,104,576]{2,1,0:T(8,128)(2,1)S(1)}, bf16[2,104,576]{2,1,0:T(8,128)(2,1)S(1)}, u32[]{:S(2)}, u32[]{:S(2)}) %collective-permute-start.26) | collective-permute-done | bytes 239648 | tf_op jit(solution)/shard_map/ppermute | solution.py:19
  407.5 6.8 %collective-permute-done.29 = bf16[2,24,3840]{2,1,0:T(8,128)(2,1)} collective-permute-done((bf16[2,24,3840]{2,1,0:T(8,128)(2,1)}, bf16[2,24,3840]{2,1,0:T(8,128)(2,1)}, u32[]{:S(2)}, u32[]{:S(2)}) %collective-permute-start.29) | collective-permute-done | bytes 368672 | tf_op jit(solution)/shard_map/ppermute | solution.py:19
  430.3 5.1 %collective-permute-done.30 = bf16[4,24,3840]{2,1,0:T(8,128)(2,1)S(1)} collective-permute-done((bf16[4,24,3840]{2,1,0:T(8,128)(2,1)S(1)}, bf16[4,24,3840]{2,1,0:T(8,128)(2,1)S(1)}, u32[]{:S(2)}, u32[]{:S(2)}) %collective-permute-start.30) | collective-permute-done | bytes 737312 | tf_op jit(solution)/shard_map/ppermute | solution.py:19
  435.4 6.0 %collective-permute-done.32 = bf16[4,24,3840]{2,1,0:T(8,128)(2,1)S(1)} collective-permute-done((bf16[4,24,3840]{2,1,0:T(8,128)(2,1)S(1)}, bf16[4,24,3840]{2,1,0:T(8,128)(2,1)S(1)}, u32[]{:S(2)}, u32[]{:S(2)}) %collective-permute-start.32) | collective-permute-done | bytes 737312 | tf_op jit(solution)/shard_map/ppermute | solution.py:19
  443.9 16.1 %collective-permute-done.33 = bf16[2,24,3840]{2,1,0:T(8,128)(2,1)S(1)} collective-permute-done((bf16[2,24,3840]{2,1,0:T(8,128)(2,1)S(1)}, bf16[2,24,3840]{2,1,0:T(8,128)(2,1)S(1)}, u32[]{:S(2)}, u32[]{:S(2)}) %collective-permute-start.33) | collective-permute-done | bytes 368672 | tf_op jit(solution)/shard_map/ppermute | solution.py:19
  460.9 4.9 %collective-permute-done.34 = bf16[24,3840]{1,0:T(8,128)(2,1)S(1)} collective-permute-done((bf16[24,3840]{1,0:T(8,128)(2,1)S(1)}, bf16[24,3840]{1,0:T(8,128)(2,1)S(1)}, u32[]{:S(2)}, u32[]{:S(2)}) %collective-permute-start.34) | collective-permute-done | bytes 184352 | tf_op jit(solution)/shard_map/ppermute | solution.py:19
  (288 shorter events, 172.1 us)
Async XLA Ops:
  11.2 15.1 %collective-permute-start.7 = (bf16[1,24,3840]{2,1,0:T(8,128)(2,1)S(1)}, bf16[1,24,3840]{2,1,0:T(8,128)(2,1)S(1)}, u32[]{:S(2)}, u32[]{:S(2)}) collective-permute-start(bf16[1,24,3840]{2,1,0:T(8,128)(2,1)S(1)} %maximum_bitcast_fusion), channel_id=1, source_target_pairs={{0,8},{1,9},{2,10},{3,11},{4,12},{5,13},{6,14},{7,15},{8,0},{9,1},... | collective-permute-start | bytes 552968 | tf_op jit(solution)/shard_map/ppermute | solution.py:19
  17.7 30.2 %collective-permute-start.1 = (bf16[2,104,576]{2,1,0:T(8,128)(2,1)S(1)}, bf16[2,104,576]{2,1,0:T(8,128)(2,1)S(1)}, u32[]{:S(2)}, u32[]{:S(2)}) collective-permute-start(bf16[2,104,576]{2,1,0:T(8,128)(2,1)S(1)} %pad_maximum_fusion.11), channel_id=1, source_target_pairs={{0,16},{1,17},{2,18},{3,19},{4,20},{5,21},{6,22},{7,23},{8,24},{9,... | collective-permute-start | bytes 718856 | tf_op jit(solution)/shard_map/ppermute | solution.py:19
  24.2 30.0 %collective-permute-start.15 = (bf16[2,96,768]{2,1,0:T(8,128)(2,1)S(1)}, bf16[2,96,768]{2,1,0:T(8,128)(2,1)S(1)}, u32[]{:S(2)}, u32[]{:S(2)}) collective-permute-start(bf16[2,96,768]{2,1,0:T(8,128)(2,1)S(1)} %pad_maximum_fusion.10), channel_id=1, source_target_pairs={{0,16},{1,17},{2,18},{3,19},{4,20},{5,21},{6,22},{7,23},{8,24},{9,... | collective-permute-start | bytes 884744 | tf_op jit(solution)/shard_map/ppermute | solution.py:19
  26.3 33.9 %collective-permute-start.8 = (bf16[2,24,3840]{2,1,0:T(8,128)(2,1)S(1)}, bf16[2,24,3840]{2,1,0:T(8,128)(2,1)S(1)}, u32[]{:S(2)}, u32[]{:S(2)}) collective-permute-start(bf16[2,24,3840]{2,1,0:T(8,128)(2,1)S(1)} %pad_maximum_fusion.9), channel_id=1, source_target_pairs={{0,16},{1,17},{2,18},{3,19},{4,20},{5,21},{6,22},{7,23},{8,24},{9,... | collective-permute-start | bytes 1105928 | tf_op jit(solution)/shard_map/ppermute | solution.py:19
  48.0 15.1 %collective-permute-start.2 = (bf16[4,104,576]{2,1,0:T(8,128)(2,1)S(1)}, bf16[4,104,576]{2,1,0:T(8,128)(2,1)S(1)}, u32[]{:S(2)}, u32[]{:S(2)}) collective-permute-start(bf16[4,104,576]{2,1,0:T(8,128)(2,1)S(1)} %pad_maximum_fusion.6), channel_id=1, source_target_pairs={{0,4},{1,5},{2,6},{3,7},{4,0},{5,1},{6,2},{7,3},{8,12},{9,13},{10,... | collective-permute-start | bytes 1437704 | tf_op jit(solution)/shard_map/ppermute | solution.py:19
  49.6 15.0 %collective-permute-start.3 = (bf16[4,104,576]{2,1,0:T(8,128)(2,1)S(1)}, bf16[4,104,576]{2,1,0:T(8,128)(2,1)S(1)}, u32[]{:S(2)}, u32[]{:S(2)}) collective-permute-start(bf16[4,104,576]{2,1,0:T(8,128)(2,1)S(1)} %pad_maximum_fusion.6), channel_id=1, source_target_pairs={{0,2},{1,3},{2,0},{3,1},{4,6},{5,7},{6,4},{7,5},{8,10},{9,11},{10,... | collective-permute-start | bytes 1437704 | tf_op jit(solution)/shard_map/ppermute | solution.py:19
  54.3 21.4 %collective-permute-start.16 = (bf16[4,96,768]{2,1,0:T(8,128)(2,1)S(1)}, bf16[4,96,768]{2,1,0:T(8,128)(2,1)S(1)}, u32[]{:S(2)}, u32[]{:S(2)}) collective-permute-start(bf16[4,96,768]{2,1,0:T(8,128)(2,1)S(1)} %pad_maximum_fusion.3), channel_id=1, source_target_pairs={{0,4},{1,5},{2,6},{3,7},{4,0},{5,1},{6,2},{7,3},{8,12},{9,13},{10,... | collective-permute-start | bytes 1769480 | tf_op jit(solution)/shard_map/ppermute | solution.py:19
  55.9 21.4 %collective-permute-start.17 = (bf16[4,96,768]{2,1,0:T(8,128)(2,1)S(1)}, bf16[4,96,768]{2,1,0:T(8,128)(2,1)S(1)}, u32[]{:S(2)}, u32[]{:S(2)}) collective-permute-start(bf16[4,96,768]{2,1,0:T(8,128)(2,1)S(1)} %pad_maximum_fusion.3), channel_id=1, source_target_pairs={{0,2},{1,3},{2,0},{3,1},{4,6},{5,7},{6,4},{7,5},{8,10},{9,11},{10,... | collective-permute-start | bytes 1769480 | tf_op jit(solution)/shard_map/ppermute | solution.py:19
  60.3 37.3 %collective-permute-start.9 = (bf16[4,24,3840]{2,1,0:T(8,128)(2,1)S(1)}, bf16[4,24,3840]{2,1,0:T(8,128)(2,1)S(1)}, u32[]{:S(2)}, u32[]{:S(2)}) collective-permute-start(bf16[4,24,3840]{2,1,0:T(8,128)(2,1)S(1)} %pad_maximum_fusion), channel_id=1, source_target_pairs={{0,4},{1,5},{2,6},{3,7},{4,0},{5,1},{6,2},{7,3},{8,12},{9,13},{10,... | collective-permute-start | bytes 2211848 | tf_op jit(solution)/shard_map/ppermute | solution.py:19
  63.1 36.0 %collective-permute-start.10 = (bf16[4,24,3840]{2,1,0:T(8,128)(2,1)S(1)}, bf16[4,24,3840]{2,1,0:T(8,128)(2,1)S(1)}, u32[]{:S(2)}, u32[]{:S(2)}) collective-permute-start(bf16[4,24,3840]{2,1,0:T(8,128)(2,1)S(1)} %pad_maximum_fusion), channel_id=1, source_target_pairs={{0,2},{1,3},{2,0},{3,1},{4,6},{5,7},{6,4},{7,5},{8,10},{9,11},{10,... | collective-permute-start | bytes 2211848 | tf_op jit(solution)/shard_map/ppermute | solution.py:19
  64.6 32.2 %collective-permute-start.4 = (bf16[2,104,576]{2,1,0:T(8,128)(2,1)S(1)}, bf16[2,104,576]{2,1,0:T(8,128)(2,1)S(1)}, u32[]{:S(2)}, u32[]{:S(2)}) collective-permute-start(bf16[2,104,576]{2,1,0:T(8,128)(2,1)S(1)} %slice.334), channel_id=1, source_target_pairs={{0,2},{1,3},{2,0},{3,1},{4,6},{5,7},{6,4},{7,5},{8,10},{9,11},{10,... | collective-permute-start | bytes 718856 | tf_op jit(solution)/shard_map/ppermute | solution.py:19
  75.7 21.7 %collective-permute-start.5 = (bf16[2,104,576]{2,1,0:T(8,128)(2,1)S(1)}, bf16[2,104,576]{2,1,0:T(8,128)(2,1)S(1)}, u32[]{:S(2)}, u32[]{:S(2)}) collective-permute-start(bf16[2,104,576]{2,1,0:T(8,128)(2,1)S(1)} %slice.335), channel_id=1, source_target_pairs={{0,4},{1,5},{2,6},{3,7},{4,0},{5,1},{6,2},{7,3},{8,12},{9,13},{10,... | collective-permute-start | bytes 718856 | tf_op jit(solution)/shard_map/ppermute | solution.py:19
  77.3 25.3 %collective-permute-start.18 = (bf16[2,96,768]{2,1,0:T(8,128)(2,1)S(1)}, bf16[2,96,768]{2,1,0:T(8,128)(2,1)S(1)}, u32[]{:S(2)}, u32[]{:S(2)}) collective-permute-start(bf16[2,96,768]{2,1,0:T(8,128)(2,1)S(1)} %slice.343), channel_id=1, source_target_pairs={{0,2},{1,3},{2,0},{3,1},{4,6},{5,7},{6,4},{7,5},{8,10},{9,11},{10,... | collective-permute-start | bytes 884744 | tf_op jit(solution)/shard_map/ppermute | solution.py:19
  97.5 14.8 %collective-permute-start.6 = (bf16[16,104,576]{2,1,0:T(8,128)(2,1)S(1)}, bf16[16,104,576]{2,1,0:T(8,128)(2,1)S(1)}, u32[]{:S(2)}, u32[]{:S(2)}) collective-permute-start(bf16[16,104,576]{2,1,0:T(8,128)(2,1)S(1)} %constant_dynamic-update-slice_fusion.mine_ref), channel_id=1, source_target_pairs={{0,1},{1,0},{2,3},{3,2},{4,5},{5,4},{6,7},{7,6},{8,9},{9,8},{10,11... | collective-permute-start | bytes 5750792 | tf_op jit(solution)/shard_map/ppermute | solution.py:19
  105.8 65.0 %collective-permute-start.20 = (bf16[16,96,768]{2,1,0:T(8,128)(2,1)}, bf16[16,96,768]{2,1,0:T(8,128)(2,1)}, u32[]{:S(2)}, u32[]{:S(2)}) collective-permute-start(bf16[16,96,768]{2,1,0:T(8,128)(2,1)} %constant_dynamic-update-slice_fusion.14.mine_ref), channel_id=1, source_target_pairs={{0,1},{1,0},{2,3},{3,2},{4,5},{5,4},{6,7},{7,6},{8,9},{9,8},{10,11... | collective-permute-start | bytes 7077896 | tf_op jit(solution)/shard_map/ppermute | solution.py:19
  112.2 63.4 %collective-permute-start.13 = (bf16[16,24,3840]{2,1,0:T(8,128)(2,1)}, bf16[16,24,3840]{2,1,0:T(8,128)(2,1)}, u32[]{:S(2)}, u32[]{:S(2)}) collective-permute-start(bf16[16,24,3840]{2,1,0:T(8,128)(2,1)} %constant_dynamic-update-slice_fusion.7.mine_ref), channel_id=1, source_target_pairs={{0,1},{1,0},{2,3},{3,2},{4,5},{5,4},{6,7},{7,6},{8,9},{9,8},{10,11... | collective-permute-start | bytes 8847368 | tf_op jit(solution)/shard_map/ppermute | solution.py:19
  330.3 26.0 %collective-permute-start.21 = (bf16[16,104,576]{2,1,0:T(8,128)(2,1)}, bf16[16,104,576]{2,1,0:T(8,128)(2,1)}, u32[]{:S(2)}, u32[]{:S(2)}) collective-permute-start(bf16[16,104,576]{2,1,0:T(8,128)(2,1)} %get-tuple-element.29), channel_id=1, source_target_pairs={{0,1},{1,0},{2,3},{3,2},{4,5},{5,4},{6,7},{7,6},{8,9},{9,8},{10,11... | collective-permute-start | bytes 5750792 | tf_op jit(solution)/shard_map/ppermute | solution.py:19
  346.1 26.2 %collective-permute-start.35 = (bf16[16,96,768]{2,1,0:T(8,128)(2,1)}, bf16[16,96,768]{2,1,0:T(8,128)(2,1)}, u32[]{:S(2)}, u32[]{:S(2)}) collective-permute-start(bf16[16,96,768]{2,1,0:T(8,128)(2,1)} %get-tuple-element.33), channel_id=1, source_target_pairs={{0,1},{1,0},{2,3},{3,2},{4,5},{5,4},{6,7},{7,6},{8,9},{9,8},{10,11... | collective-permute-start | bytes 7077896 | tf_op jit(solution)/shard_map/ppermute | solution.py:19
  369.6 31.0 %collective-permute-start.28 = (bf16[16,24,3840]{2,1,0:T(8,128)(2,1)}, bf16[16,24,3840]{2,1,0:T(8,128)(2,1)S(1)}, u32[]{:S(2)}, u32[]{:S(2)}) collective-permute-start(bf16[16,24,3840]{2,1,0:T(8,128)(2,1)} %get-tuple-element.31), channel_id=1, source_target_pairs={{0,1},{1,0},{2,3},{3,2},{4,5},{5,4},{6,7},{7,6},{8,9},{9,8},{10,11... | collective-permute-start | bytes 8847368 | tf_op jit(solution)/shard_map/ppermute | solution.py:19
  370.0 15.0 %collective-permute-start.23 = (bf16[4,104,576]{2,1,0:T(8,128)(2,1)S(1)}, bf16[4,104,576]{2,1,0:T(8,128)(2,1)S(1)}, u32[]{:S(2)}, u32[]{:S(2)}) collective-permute-start(bf16[4,104,576]{2,1,0:T(8,128)(2,1)S(1)} %pad_maximum_fusion.7), channel_id=1, source_target_pairs={{0,4},{1,5},{2,6},{3,7},{4,0},{5,1},{6,2},{7,3},{8,12},{9,13},{10,... | collective-permute-start | bytes 1437704 | tf_op jit(solution)/shard_map/ppermute | solution.py:19
  371.6 15.0 %collective-permute-start.25 = (bf16[4,104,576]{2,1,0:T(8,128)(2,1)S(1)}, bf16[4,104,576]{2,1,0:T(8,128)(2,1)S(1)}, u32[]{:S(2)}, u32[]{:S(2)}) collective-permute-start(bf16[4,104,576]{2,1,0:T(8,128)(2,1)S(1)} %pad_maximum_fusion.8), channel_id=1, source_target_pairs={{0,2},{1,3},{2,0},{3,1},{4,6},{5,7},{6,4},{7,5},{8,10},{9,11},{10,... | collective-permute-start | bytes 1437704 | tf_op jit(solution)/shard_map/ppermute | solution.py:19
  374.9 17.3 %collective-permute-start.36 = (bf16[2,96,768]{2,1,0:T(8,128)(2,1)S(1)}, bf16[2,96,768]{2,1,0:T(8,128)(2,1)S(1)}, u32[]{:S(2)}, u32[]{:S(2)}) collective-permute-start(bf16[2,96,768]{2,1,0:T(8,128)(2,1)S(1)} %get-tuple-element.91), channel_id=1, source_target_pairs={{0,2},{1,3},{2,0},{3,1},{4,6},{5,7},{6,4},{7,5},{8,10},{9,11},{10,... | collective-permute-start | bytes 884744 | tf_op jit(solution)/shard_map/ppermute | solution.py:19
  376.4 15.8 %collective-permute-start.38 = (bf16[2,96,768]{2,1,0:T(8,128)(2,1)S(1)}, bf16[2,96,768]{2,1,0:T(8,128)(2,1)S(1)}, u32[]{:S(2)}, u32[]{:S(2)}) collective-permute-start(bf16[2,96,768]{2,1,0:T(8,128)(2,1)S(1)} %get-tuple-element.92), channel_id=1, source_target_pairs={{0,4},{1,5},{2,6},{3,7},{4,0},{5,1},{6,2},{7,3},{8,12},{9,13},{10,... | collective-permute-start | bytes 884744 | tf_op jit(solution)/shard_map/ppermute | solution.py:19
  386.9 13.6 %collective-permute-start.26 = (bf16[2,104,576]{2,1,0:T(8,128)(2,1)S(1)}, bf16[2,104,576]{2,1,0:T(8,128)(2,1)S(1)}, u32[]{:S(2)}, u32[]{:S(2)}) collective-permute-start(bf16[2,104,576]{2,1,0:T(8,128)(2,1)S(1)} %slice.456), channel_id=1, source_target_pairs={{0,16},{1,17},{2,18},{3,19},{4,20},{5,21},{6,22},{7,23},{8,24},{9,... | collective-permute-start | bytes 718856 | tf_op jit(solution)/shard_map/ppermute | solution.py:19
  393.3 29.2 %collective-permute-start.37 = (bf16[4,96,768]{2,1,0:T(8,128)(2,1)}, bf16[4,96,768]{2,1,0:T(8,128)(2,1)}, u32[]{:S(2)}, u32[]{:S(2)}) collective-permute-start(bf16[4,96,768]{2,1,0:T(8,128)(2,1)} %pad_maximum_fusion.4), channel_id=1, source_target_pairs={{0,4},{1,5},{2,6},{3,7},{4,0},{5,1},{6,2},{7,3},{8,12},{9,13},{10,... | collective-permute-start | bytes 1769480 | tf_op jit(solution)/shard_map/ppermute | solution.py:19
  403.0 13.1 %collective-permute-start.31 = (bf16[2,24,3840]{2,1,0:T(8,128)(2,1)}, bf16[2,24,3840]{2,1,0:T(8,128)(2,1)}, u32[]{:S(2)}, u32[]{:S(2)}) collective-permute-start(bf16[2,24,3840]{2,1,0:T(8,128)(2,1)} %get-tuple-element.86), channel_id=1, source_target_pairs={{0,4},{1,5},{2,6},{3,7},{4,0},{5,1},{6,2},{7,3},{8,12},{9,13},{10,... | collective-permute-start | bytes 1105928 | tf_op jit(solution)/shard_map/ppermute | solution.py:19
  404.4 22.5 %collective-permute-start.39 = (bf16[4,96,768]{2,1,0:T(8,128)(2,1)}, bf16[4,96,768]{2,1,0:T(8,128)(2,1)}, u32[]{:S(2)}, u32[]{:S(2)}) collective-permute-start(bf16[4,96,768]{2,1,0:T(8,128)(2,1)} %pad_maximum_fusion.5), channel_id=1, source_target_pairs={{0,2},{1,3},{2,0},{3,1},{4,6},{5,7},{6,4},{7,5},{8,10},{9,11},{10,... | collective-permute-start | bytes 1769480 | tf_op jit(solution)/shard_map/ppermute | solution.py:19
  418.5 16.9 %collective-permute-start.30 = (bf16[4,24,3840]{2,1,0:T(8,128)(2,1)S(1)}, bf16[4,24,3840]{2,1,0:T(8,128)(2,1)S(1)}, u32[]{:S(2)}, u32[]{:S(2)}) collective-permute-start(bf16[4,24,3840]{2,1,0:T(8,128)(2,1)S(1)} %pad_maximum_fusion.1), channel_id=1, source_target_pairs={{0,4},{1,5},{2,6},{3,7},{4,0},{5,1},{6,2},{7,3},{8,12},{9,13},{10,... | collective-permute-start | bytes 2211848 | tf_op jit(solution)/shard_map/ppermute | solution.py:19
  419.1 22.2 %collective-permute-start.32 = (bf16[4,24,3840]{2,1,0:T(8,128)(2,1)S(1)}, bf16[4,24,3840]{2,1,0:T(8,128)(2,1)S(1)}, u32[]{:S(2)}, u32[]{:S(2)}) collective-permute-start(bf16[4,24,3840]{2,1,0:T(8,128)(2,1)S(1)} %pad_maximum_fusion.2), channel_id=1, source_target_pairs={{0,2},{1,3},{2,0},{3,1},{4,6},{5,7},{6,4},{7,5},{8,10},{9,11},{10,... | collective-permute-start | bytes 2211848 | tf_op jit(solution)/shard_map/ppermute | solution.py:19
  428.5 14.9 %collective-permute-start.40 = (bf16[2,96,768]{2,1,0:T(8,128)(2,1)S(1)}, bf16[2,96,768]{2,1,0:T(8,128)(2,1)S(1)}, u32[]{:S(2)}, u32[]{:S(2)}) collective-permute-start(bf16[2,96,768]{2,1,0:T(8,128)(2,1)S(1)} %slice.455), channel_id=1, source_target_pairs={{0,16},{1,17},{2,18},{3,19},{4,20},{5,21},{6,22},{7,23},{8,24},{9,... | collective-permute-start | bytes 884744 | tf_op jit(solution)/shard_map/ppermute | solution.py:19
  441.7 18.3 %collective-permute-start.33 = (bf16[2,24,3840]{2,1,0:T(8,128)(2,1)S(1)}, bf16[2,24,3840]{2,1,0:T(8,128)(2,1)S(1)}, u32[]{:S(2)}, u32[]{:S(2)}) collective-permute-start(bf16[2,24,3840]{2,1,0:T(8,128)(2,1)S(1)} %slice.454), channel_id=1, source_target_pairs={{0,16},{1,17},{2,18},{3,19},{4,20},{5,21},{6,22},{7,23},{8,24},{9,... | collective-permute-start | bytes 1105928 | tf_op jit(solution)/shard_map/ppermute | solution.py:19
  443.5 16.6 %collective-permute-start.41 = (bf16[96,768]{1,0:T(8,128)(2,1)S(1)}, bf16[96,768]{1,0:T(8,128)(2,1)S(1)}, u32[]{:S(2)}, u32[]{:S(2)}) collective-permute-start(bf16[96,768]{1,0:T(8,128)(2,1)S(1)} %fusion.36), channel_id=1, source_target_pairs={{0,8},{1,9},{2,10},{3,11},{4,12},{5,13},{6,14},{7,15},{8,0},{9,1},... | collective-permute-start | bytes 442376 | tf_op jit(solution)/shard_map/ppermute | solution.py:19
  (48 other events, 558.1 us)
